TPU v7x, 32 devices: a whole 2x2x4 slice. The times are simulated.
32 devices in a mesh: grp: 4 (over y, x), ep: 8 (over z, core).
Axes of the slice: x: 2, y: 2, z: 4, core: 2. Of those that a mesh axis runs over, the one named last changes fastest.
Arguments:
- layer_in: bfloat16 [4096, 1536], P(('grp', 'ep')), may hold values from -6 to 6
- segments: int32 [4096], P(('grp', 'ep')), may hold values from 0 to 4, as said below
- routes: int32 [4096, 8], P(('grp', 'ep')), may hold values from 0 to 23, all different within a row; in each aligned block of 128 rows (0 to 127, 128 to 255, ...) at most 56 rows name the same one
- qkv_weight: bfloat16 [2560, 1536], P('ep'), may hold values from -0.15625 to 0.15625
- out_weight: bfloat16 [1536, 1536], P('ep'), may hold values from -1.25 to 1.25
- router_weight: bfloat16 [24, 1536], P('ep'), may hold values from -0.078125 to 0.078125
- norm1_gain: bfloat16 [1536], P('ep'), may hold values from 0.25 to 1.75
- norm2_gain: bfloat16 [1536], P('ep'), may hold values from 0.25 to 1.75
- w_gate: bfloat16 [24, 512, 1536], P('ep'), may hold values from -0.15625 to 0.15625
- w_up: bfloat16 [24, 512, 1536], P('ep'), may hold values from -0.15625 to 0.15625
- w_down: bfloat16 [24, 512, 1536], P('ep'), may hold values from -1 to 1
- out_cotangent: bfloat16 [4096, 1536], P(('grp', 'ep')), may hold values from -6 to 6
Outputs:
- layer_out: bfloat16 [4096, 1536], P(('grp', 'ep'))
- grad_in: bfloat16 [4096, 1536], P(('grp', 'ep'))
- grad_qkv: float32 [2560, 1536], P('ep')
- grad_out_weight: float32 [1536, 1536], P('ep')
- grad_router: float32 [24, 1536], P('ep')
- grad_norm1: float32 [1536], P('ep')
- grad_norm2: float32 [1536], P('ep')
- grad_gate: float32 [24, 512, 1536], P('ep', None, 'grp')
- grad_up: float32 [24, 512, 1536], P('ep', None, 'grp')
- grad_down: float32 [24, 512, 1536], P('ep', None, 'grp')
Inputs may be any that keep to these rules, and one draw needn't show every extreme that they name: `segments`: within each sequence of 1024 tokens the numbers start at 0 and rise by one at each new document. Every document has at most 800 tokens and each sequence holds one of exactly 800; every document but a sequence's last has 60 or more. `routes`: each row names 8 different experts. In the rows of one device (128 aligned rows) no expert is named by more than 56 rows, a bound that some block reaches.
All inputs are finite; a program needn't handle non-finite values.
Results may differ from a plain program's by a relative error of at most 0.025.
Values may be sent and summed in bfloat16 or wider, within the bound.
No kernel may reach another device: no remote copies, remote signals or barrier semaphores. Data moves between devices by JAX's collectives and lax.ppermute only.
A program may use at most 192 MiB of HBM per device.

v0:
```python
import math

import jax
import jax.numpy as jnp
from jax import lax
from jax.sharding import PartitionSpec as P

QUERY_HEADS = 24
KEY_VALUE_HEADS = 8
HEAD_DIMENSION = 64
TOPK = 8


eps = 1e-06
theta = 10000.0
negative_large = -1e30


def angles(token_positions, head_size):
    half = head_size // 2
    freq = theta ** (-jnp.arange(half, dtype=jnp.float32) * 2.0 / head_size)
    angle = token_positions.astype(jnp.float32)[:, None] * freq[None, :]
    return (jnp.cos(angle)[:, None, :], jnp.sin(angle)[:, None, :])


def rotate(value_matrix, cosine_table, sine_table):
    half = value_matrix.shape[-1] // 2
    leading_entry = value_matrix[..., :half]
    second = value_matrix[..., half:]
    return jnp.concatenate(
        [
            leading_entry * cosine_table - second * sine_table,
            second * cosine_table + leading_entry * sine_table,
        ],
        axis=-1,
    )


def inverse_rotation(grads, cosine_table, sine_table):
    half = grads.shape[-1] // 2
    leading_entry = grads[..., :half]
    second = grads[..., half:]
    return jnp.concatenate(
        [
            leading_entry * cosine_table + second * sine_table,
            second * cosine_table - leading_entry * sine_table,
        ],
        axis=-1,
    )


def norm_back(delta, normed, scale, gain):
    gain_grad = jnp.sum(delta * normed, axis=0)
    scaled = delta * gain
    back = scale * (scaled - normed * jnp.mean(scaled * normed, axis=-1, keepdims=True))
    return (back, gain_grad)


def local(
    layer_in,
    segments,
    routes,
    qkv_weight,
    out_weight,
    router_weight,
    norm1_gain,
    norm2_gain,
    w_gate,
    w_up,
    w_down,
    out_cotangent,
):
    token_stream, width = layer_in.shape
    group_size = lax.axis_size("ep")
    group_rank = lax.axis_index("ep")
    local_count = w_gate.shape[0]
    experts = local_count * group_size
    seq_len = token_stream * group_size
    query_span_width = QUERY_HEADS * HEAD_DIMENSION
    key_span_width = KEY_VALUE_HEADS * HEAD_DIMENSION
    head_group = QUERY_HEADS // KEY_VALUE_HEADS
    send_rows = 8 * ((5 * token_stream * TOPK + 32 * experts - 1) // (32 * experts))
    capacity = 9 * token_stream * TOPK // (8 * local_count)
    pairs = token_stream * TOPK
    scale = HEAD_DIMENSION ** (-0.5)
    full_qkv, full_out, full_router, gain_one, gain_two = (
        lax.all_gather(qkv_weight, "ep", axis=0, tiled=True),
        lax.all_gather(out_weight, "ep", axis=0, tiled=True),
        lax.all_gather(router_weight, "ep", axis=0, tiled=True),
        lax.all_gather(norm1_gain, "ep", axis=0, tiled=True),
        lax.all_gather(norm2_gain, "ep", axis=0, tiled=True),
    )
    residual = layer_in.astype(jnp.float32)
    scale_one = lax.rsqrt(jnp.mean(residual * residual, axis=-1, keepdims=True) + eps)
    normed_one = residual * scale_one
    x_low = (normed_one * gain_one).astype(jnp.bfloat16)
    projected_rows = jnp.einsum("td,cd->tc", x_low, full_qkv, preferred_element_type=jnp.float32)
    token_positions = group_rank * token_stream + jnp.arange(token_stream, dtype=jnp.int32)
    cosine_table, sine_table = angles(token_positions, HEAD_DIMENSION)
    query_matrix = rotate(
        projected_rows[:, :query_span_width].reshape(token_stream, QUERY_HEADS, HEAD_DIMENSION),
        cosine_table,
        sine_table,
    ).astype(jnp.bfloat16)
    query_matrix = query_matrix.reshape(token_stream, KEY_VALUE_HEADS, head_group, HEAD_DIMENSION)
    key_matrix = rotate(
        projected_rows[:, query_span_width : query_span_width + key_span_width].reshape(
            token_stream, KEY_VALUE_HEADS, HEAD_DIMENSION
        ),
        cosine_table,
        sine_table,
    )
    key_matrix = key_matrix.astype(jnp.bfloat16).reshape(token_stream, key_span_width)
    value_matrix = projected_rows[:, query_span_width + key_span_width :].astype(jnp.bfloat16)
    seg_rows = segments.astype(jnp.bfloat16)

    def key_block(piece, leading_entry, tile_block):
        key_lines, value_lines, key_seg = piece
        key_portion = lax.dynamic_slice_in_dim(key_lines, leading_entry, tile_block, 0).reshape(
            tile_block, KEY_VALUE_HEADS, HEAD_DIMENSION
        )
        value_portion = lax.dynamic_slice_in_dim(value_lines, leading_entry, tile_block, 0).reshape(
            tile_block, KEY_VALUE_HEADS, HEAD_DIMENSION
        )
        seg_part = lax.dynamic_slice_in_dim(key_seg, leading_entry, tile_block, 0)
        key_pos = leading_entry + jnp.arange(tile_block, dtype=jnp.int32)
        valid = (seg_rows[:, None] == seg_part[None, :]) & (
            key_pos[None, :] <= token_positions[:, None]
        )
        score = (
            jnp.einsum(
                "qhgd,khd->hgqk", query_matrix, key_portion, preferred_element_type=jnp.float32
            )
            * scale
        )
        return (key_portion, value_portion, valid, score)

    start_state = (
        jnp.full((KEY_VALUE_HEADS, head_group, token_stream), negative_large, jnp.float32),
        jnp.zeros((KEY_VALUE_HEADS, head_group, token_stream), jnp.float32),
        jnp.zeros((KEY_VALUE_HEADS, head_group, token_stream, HEAD_DIMENSION), jnp.float32),
    )
    carry = start_state
    piece = (
        lax.all_gather(key_matrix, "ep", axis=0, tiled=True),
        lax.all_gather(value_matrix, "ep", axis=0, tiled=True),
        lax.all_gather(seg_rows, "ep", axis=0, tiled=True),
    )
    count = piece[0].shape[0]
    tile_block = math.gcd(count, 512)

    def step(state, index):
        top, total, weighted = state
        leading_entry = index * tile_block
        key_portion, value_portion, valid, score = key_block(piece, leading_entry, tile_block)
        score = jnp.where(valid, score, negative_large)
        new_top = jnp.maximum(top, jnp.max(score, axis=-1))
        weight = jnp.where(valid, jnp.exp(score - new_top[..., None]), 0.0)
        factor = jnp.exp(top - new_top)
        total = total * factor + jnp.sum(weight, axis=-1)
        weighted = weighted * factor[..., None] + jnp.einsum(
            "hgqk,khd->hgqd",
            weight.astype(jnp.bfloat16),
            value_portion,
            preferred_element_type=jnp.float32,
        )
        return ((new_top, total, weighted), None)

    carry, _ = lax.scan(step, carry, jnp.arange(count // tile_block, dtype=jnp.int32))
    top, total, weighted = carry
    attn_out = weighted / total[..., None]
    log_total = top + jnp.log(total)
    mixed = (
        attn_out.transpose(2, 0, 1, 3).reshape(token_stream, query_span_width).astype(jnp.bfloat16)
    )
    branch = jnp.einsum("tc,dc->td", mixed, full_out, preferred_element_type=jnp.float32)
    hidden_one = residual + branch
    scale_two = lax.rsqrt(jnp.mean(hidden_one * hidden_one, axis=-1, keepdims=True) + eps)
    normed_two = hidden_one * scale_two
    x_two = (normed_two * gain_two).astype(jnp.bfloat16)
    logits = jnp.einsum("td,ed->te", x_two, full_router, preferred_element_type=jnp.float32)
    choose = routes[:, :, None] == jnp.arange(experts, dtype=jnp.int32)[None, None, :]
    chosen = jnp.sum(jnp.where(choose, logits[:, None, :], 0.0), axis=-1)
    gates = jax.nn.softmax(chosen, axis=-1)
    pair_expert = routes.reshape(pairs)
    marks = (pair_expert[:, None] == jnp.arange(experts, dtype=jnp.int32)[None, :]).astype(
        jnp.int32
    )
    counts = jnp.sum(marks, axis=0, dtype=jnp.int32)
    rank = jnp.sum(
        (jnp.cumsum(marks, axis=0, dtype=jnp.int32) - marks) * marks, axis=1, dtype=jnp.int32
    )
    slot = pair_expert * send_rows + rank
    owner = (
        jnp.full((experts * send_rows,), pairs, jnp.int32)
        .at[slot]
        .set(jnp.arange(pairs, dtype=jnp.int32))
    )
    filled = owner < pairs
    owner_pair = jnp.minimum(owner, pairs - 1)
    outgoing = jnp.where(filled[:, None], x_two[owner_pair // TOPK], jnp.zeros((), jnp.bfloat16))
    outgoing = outgoing.reshape(experts, send_rows, width)
    count_code = jnp.stack([counts // 16, counts % 16], axis=1).astype(jnp.bfloat16)
    incoming, code_in = (
        lax.all_to_all(outgoing, "ep", split_axis=0, concat_axis=1, tiled=True),
        lax.all_to_all(count_code, "ep", split_axis=0, concat_axis=1, tiled=True),
    )
    code_pairs = code_in.astype(jnp.int32).reshape(local_count, group_size, 2)
    source_count = code_pairs[:, :, 0] * 16 + code_pairs[:, :, 1]
    source_start = jnp.cumsum(source_count, axis=1, dtype=jnp.int32) - source_count
    source_end = source_start + source_count
    place = jnp.arange(capacity, dtype=jnp.int32)
    source = jnp.sum(
        (place[None, :, None] >= source_end[:, None, :]).astype(jnp.int32), axis=2, dtype=jnp.int32
    )
    source = jnp.minimum(source, group_size - 1)
    begin = jnp.take_along_axis(source_start, source, axis=1)
    live = place[None, :] < source_end[:, -1:]
    gather_row = source * send_rows + jnp.minimum(place[None, :] - begin, send_rows - 1)
    slot_index = jnp.arange(group_size * send_rows, dtype=jnp.int32)
    slot_source = slot_index // send_rows
    slot_offset = slot_index % send_rows
    slot_place = source_start[:, slot_source] + slot_offset[None, :]
    slot_keep = (slot_offset[None, :] < source_count[:, slot_source]) & (slot_place < capacity)
    slot_pick = jnp.minimum(slot_place, capacity - 1)

    def compact(rows):
        taken = jnp.take_along_axis(rows, gather_row[:, :, None], axis=1)
        return jnp.where(live[:, :, None], taken, jnp.zeros((), rows.dtype))

    def spread(rows):
        taken = jnp.take_along_axis(rows, slot_pick[:, :, None], axis=1)
        return jnp.where(slot_keep[:, :, None], taken, jnp.zeros((), rows.dtype))

    dense_in = compact(incoming)
    gate_pre = jnp.einsum("jcd,jfd->jcf", dense_in, w_gate, preferred_element_type=jnp.float32)
    up_pre = jnp.einsum("jcd,jfd->jcf", dense_in, w_up, preferred_element_type=jnp.float32)
    inner = (jax.nn.silu(gate_pre) * up_pre).astype(jnp.bfloat16)
    expert_out = jnp.einsum(
        "jcf,jfd->jcd", inner, w_down, preferred_element_type=jnp.float32
    ).astype(jnp.bfloat16)
    returned = lax.all_to_all(spread(expert_out), "ep", split_axis=1, concat_axis=0, tiled=True)
    pair_out = returned.reshape(experts * send_rows, width)[slot].reshape(token_stream, TOPK, width)
    expert_sum = jnp.sum(gates[:, :, None] * pair_out, axis=1)
    layer_out = (hidden_one + expert_sum).astype(jnp.bfloat16)
    delta = out_cotangent.astype(jnp.float32)
    gate_grad = jnp.sum(delta[:, None, :] * pair_out, axis=-1)
    pair_delta = (gates[:, :, None] * delta[:, None, :]).astype(jnp.bfloat16).reshape(pairs, width)
    outgoing_grad = jnp.where(filled[:, None], pair_delta[owner_pair], jnp.zeros((), jnp.bfloat16))
    outgoing_grad = outgoing_grad.reshape(experts, send_rows, width)
    incoming_grad = lax.all_to_all(outgoing_grad, "ep", split_axis=0, concat_axis=1, tiled=True)
    dense_grad = compact(incoming_grad)
    down_grad = jnp.einsum("jcf,jcd->jfd", inner, dense_grad, preferred_element_type=jnp.float32)
    inner_grad = jnp.einsum("jcd,jfd->jcf", dense_grad, w_down, preferred_element_type=jnp.float32)
    logistic = jax.nn.sigmoid(gate_pre)
    gate_back = (inner_grad * up_pre * logistic * (1.0 + gate_pre * (1.0 - logistic))).astype(
        jnp.bfloat16
    )
    up_back = (inner_grad * gate_pre * logistic).astype(jnp.bfloat16)
    gate_w_grad = jnp.einsum(
        "jcf,jcd->jfd", gate_back, dense_in, preferred_element_type=jnp.float32
    )
    up_w_grad = jnp.einsum("jcf,jcd->jfd", up_back, dense_in, preferred_element_type=jnp.float32)
    slot_grad = (
        jnp.einsum("jcf,jfd->jcd", gate_back, w_gate, preferred_element_type=jnp.float32)
        + jnp.einsum("jcf,jfd->jcd", up_back, w_up, preferred_element_type=jnp.float32)
    ).astype(jnp.bfloat16)
    back_rows = lax.all_to_all(spread(slot_grad), "ep", split_axis=1, concat_axis=0, tiled=True)
    pair_back = back_rows.reshape(experts * send_rows, width)[slot].reshape(
        token_stream, TOPK, width
    )
    two_grad = jnp.sum(pair_back.astype(jnp.float32), axis=1)
    back_qkv, back_out, back_router, back_gain_one, back_gain_two = (
        lax.all_gather(qkv_weight, "ep", axis=0, tiled=True),
        lax.all_gather(out_weight, "ep", axis=0, tiled=True),
        lax.all_gather(router_weight, "ep", axis=0, tiled=True),
        lax.all_gather(norm1_gain, "ep", axis=0, tiled=True),
        lax.all_gather(norm2_gain, "ep", axis=0, tiled=True),
    )
    chosen_grad = gates * (gate_grad - jnp.sum(gates * gate_grad, axis=-1, keepdims=True))
    logit_grad = jnp.sum(jnp.where(choose, chosen_grad[:, :, None], 0.0), axis=1).astype(
        jnp.bfloat16
    )
    router_grad = jnp.einsum("te,td->ed", logit_grad, x_two, preferred_element_type=jnp.float32)
    two_grad = two_grad + jnp.einsum(
        "te,ed->td", logit_grad, back_router, preferred_element_type=jnp.float32
    )
    norm_two_back, gain_two_grad = norm_back(two_grad, normed_two, scale_two, back_gain_two)
    hidden_grad = delta + norm_two_back
    hidden_low = hidden_grad.astype(jnp.bfloat16)
    mixing_gradient = jnp.einsum(
        "td,dc->tc", hidden_low, back_out, preferred_element_type=jnp.float32
    ).astype(jnp.bfloat16)
    output_change = mixing_gradient.reshape(
        token_stream, KEY_VALUE_HEADS, head_group, HEAD_DIMENSION
    ).transpose(1, 2, 0, 3)
    delta_rows = jnp.sum(output_change.astype(jnp.float32) * attn_out, axis=-1)
    back_state = (
        jnp.zeros((KEY_VALUE_HEADS, head_group, token_stream, HEAD_DIMENSION), jnp.float32),
        jnp.zeros((seq_len, 2 * key_span_width), jnp.float32),
    )
    carry = back_state
    attend_piece = (
        lax.all_gather(key_matrix, "ep", axis=0, tiled=True),
        lax.all_gather(value_matrix, "ep", axis=0, tiled=True),
        lax.all_gather(seg_rows, "ep", axis=0, tiled=True),
    )
    count = attend_piece[0].shape[0]
    attend_tile_block = math.gcd(count, 512)

    def step(state, index):
        query_grad, key_terms = state
        leading_entry = index * attend_tile_block
        key_portion, value_portion, valid, score = key_block(
            attend_piece, leading_entry, attend_tile_block
        )
        prob = jnp.where(valid, jnp.exp(score - log_total[..., None]), 0.0)
        value_grad = jnp.einsum(
            "hgqk,hgqd->khd",
            prob.astype(jnp.bfloat16),
            output_change,
            preferred_element_type=jnp.float32,
        )
        prob_grad = jnp.einsum(
            "hgqd,khd->hgqk", output_change, value_portion, preferred_element_type=jnp.float32
        )
        score_grad = (prob * (prob_grad - delta_rows[..., None])).astype(jnp.bfloat16)
        query_grad = (
            query_grad
            + jnp.einsum(
                "hgqk,khd->hgqd", score_grad, key_portion, preferred_element_type=jnp.float32
            )
            * scale
        )
        key_grad = (
            jnp.einsum(
                "hgqk,qhgd->khd", score_grad, query_matrix, preferred_element_type=jnp.float32
            )
            * scale
        )
        rows = jnp.concatenate(
            [
                key_grad.reshape(attend_tile_block, key_span_width),
                value_grad.reshape(attend_tile_block, key_span_width),
            ],
            axis=1,
        )
        previous = lax.dynamic_slice_in_dim(key_terms, leading_entry, attend_tile_block, 0)
        key_terms = lax.dynamic_update_slice_in_dim(key_terms, previous + rows, leading_entry, 0)
        return ((query_grad, key_terms), None)

    carry, _ = lax.scan(step, carry, jnp.arange(count // attend_tile_block, dtype=jnp.int32))
    query_grad, key_terms = carry
    key_nearby = lax.psum_scatter(
        key_terms.astype(jnp.bfloat16), "ep", scatter_dimension=0, tiled=True
    ).astype(jnp.float32)
    q_grad = inverse_rotation(
        query_grad.transpose(2, 0, 1, 3).reshape(token_stream, QUERY_HEADS, HEAD_DIMENSION),
        cosine_table,
        sine_table,
    )
    key_gradient = inverse_rotation(
        key_nearby[:, :key_span_width].reshape(token_stream, KEY_VALUE_HEADS, HEAD_DIMENSION),
        cosine_table,
        sine_table,
    )
    proj_grad = jnp.concatenate(
        [
            q_grad.reshape(token_stream, query_span_width),
            key_gradient.reshape(token_stream, key_span_width),
            key_nearby[:, key_span_width:],
        ],
        axis=1,
    ).astype(jnp.bfloat16)
    one_grad = jnp.einsum("tc,cd->td", proj_grad, back_qkv, preferred_element_type=jnp.float32)
    norm_one_back, gain_one_grad = norm_back(one_grad, normed_one, scale_one, back_gain_one)
    grad_in = (hidden_grad + norm_one_back).astype(jnp.bfloat16)
    qkv_grad = jnp.einsum("tc,td->cd", proj_grad, x_low, preferred_element_type=jnp.float32)
    out_grad = jnp.einsum("td,tc->dc", hidden_low, mixed, preferred_element_type=jnp.float32)
    qkv_part, out_part, router_part, gain_one_part, gain_two_part = (
        lax.psum_scatter(
            qkv_grad.astype(jnp.bfloat16), "ep", scatter_dimension=0, tiled=True
        ).astype(jnp.float32),
        lax.psum_scatter(
            out_grad.astype(jnp.bfloat16), "ep", scatter_dimension=0, tiled=True
        ).astype(jnp.float32),
        lax.psum_scatter(
            router_grad.astype(jnp.bfloat16), "ep", scatter_dimension=0, tiled=True
        ).astype(jnp.float32),
        lax.psum_scatter(
            gain_one_grad.astype(jnp.bfloat16), "ep", scatter_dimension=0, tiled=True
        ).astype(jnp.float32),
        lax.psum_scatter(
            gain_two_grad.astype(jnp.bfloat16), "ep", scatter_dimension=0, tiled=True
        ).astype(jnp.float32),
    )
    total_sums = (
        lax.psum(qkv_part.astype(jnp.bfloat16), "grp").astype(jnp.float32),
        lax.psum(out_part.astype(jnp.bfloat16), "grp").astype(jnp.float32),
        lax.psum(router_part.astype(jnp.bfloat16), "grp").astype(jnp.float32),
        lax.psum(gain_one_part.astype(jnp.bfloat16), "grp").astype(jnp.float32),
        lax.psum(gain_two_part.astype(jnp.bfloat16), "grp").astype(jnp.float32),
    )
    expert_sums = (
        lax.psum_scatter(
            gate_w_grad.astype(jnp.bfloat16), "grp", scatter_dimension=2, tiled=True
        ).astype(jnp.float32),
        lax.psum_scatter(
            up_w_grad.astype(jnp.bfloat16), "grp", scatter_dimension=2, tiled=True
        ).astype(jnp.float32),
        lax.psum_scatter(
            down_grad.astype(jnp.bfloat16), "grp", scatter_dimension=2, tiled=True
        ).astype(jnp.float32),
    )
    return (
        layer_out,
        grad_in,
        total_sums[0],
        total_sums[1],
        total_sums[2],
        total_sums[3],
        total_sums[4],
        expert_sums[0],
        expert_sums[1],
        expert_sums[2],
    )


def solution(mesh):
    in_specs = (
        P(("grp", "ep"), None),
        P(("grp", "ep")),
        P(("grp", "ep"), None),
        P("ep", None),
        P("ep", None),
        P("ep", None),
        P("ep"),
        P("ep"),
        P("ep", None, None),
        P("ep", None, None),
        P("ep", None, None),
        P(("grp", "ep"), None),
    )
    out_specs = (
        P(("grp", "ep"), None),
        P(("grp", "ep"), None),
        P("ep", None),
        P("ep", None),
        P("ep", None),
        P("ep"),
        P("ep"),
        P("ep", None, "grp"),
        P("ep", None, "grp"),
        P("ep", None, "grp"),
    )
    return jax.shard_map(local, mesh=mesh, in_specs=in_specs, out_specs=out_specs, check_vma=False)
```

profile of v0, /device:TPU:16, one launch (start us, length us, event | category | flops | bytes accessed | tf_op | source)
XLA Modules:
  0.0 1410.2 jit_solution(10302426742077891368)
XLA Ops:
  11.7 11.8 all-reduce.6
  24.7 62.4 %all-gather.7.cloned.1.call-done = bf16[2560,1536]{1,0:T(8,128)(2,1)} async-done(((bf16[320,1536]{1,0:T(8,128)(2,1)}), bf16[2560,1536]{1,0:T(8,128)(2,1)}) %all-gather.7.cloned.1.call-update) | async-done | bytes 7864336 | tf_op jit(solution)/shard_map/all_gather | solution.py:87
  109.3 12.2 all-gather.1
  128.3 10.9 all-gather
  142.7 29.2 %while.28 = (s32[]{:T(128)}, f32[8,3,128]{2,1,0:T(4,128)S(1)}, f32[8,3,128]{2,1,0:T(4,128)S(1)}, f32[8,3,128,64]{2,3,1,0:T(8,128)S(1)}, bf16[128]{0:T(256)(128)(...) while((s32[]{:T(128)}, f32[8,3,128]{2,1,0:T(4,128)S(1)}, ...), condition=%wide.region_4.5_spmd.clone, body=%wide.region_1.4_spmd.clone.sunk | while | flops 424033920 | bytes 49619452 | solution.py:169
  172.0 20.3 %all-gather.13.cloned.1.call-done = bf16[1536,1536]{1,0:T(8,128)(2,1)} async-done(((bf16[192,1536]{1,0:T(8,128)(2,1)}), bf16[1536,1536]{1,0:T(8,128)(2,1)}) %all-gather.13.cloned.1.call-update) | async-done | bytes 4718608 | tf_op jit(solution)/shard_map/all_gather | solution.py:88
  218.5 95.6 %all_to_all.76 = bf16[24,56,1536]{2,1,0:T(8,128)(2,1)} all-to-all(bf16[24,56,1536]{2,1,0:T(8,128)(2,1)} %get-tuple-element.492), channel_id=1, replica_groups=mesh['grp'=4,'ep'=8] {'ep'}, dimensions={0} | all-to-all | bytes 8257536 | tf_op jit(solution)/shard_map/all_to_all | solution.py:251
  314.1 8.0 all-to-all-start.1
  336.6 74.8 %all-to-all-done.1 = bf16[24,56,1536]{2,1,0:T(8,128)(2,1)} async-done(((bf16[24,56,1536]{2,1,0:T(8,128)(2,1)}), bf16[24,56,1536]{2,1,0:T(8,128)(2,1)}, u32[]{:S(2)}, u32[]{:S(2)}) %all-to-all-start.1) | async-done | bytes 4128800 | tf_op jit(solution)/shard_map/all_to_all | solution.py:205
  415.9 26.7 %gather_fusion.9 = bf16[1152,1536]{1,0:T(8,128)(2,1)} fusion(bf16[3,448,1536]{2,1,0:T(8,128)(2,1)} %bitcast.267, s32[1152]{0:T(1024)S(1)} %reshape.789), kind=kCustom, calls=%fused_computation.2.clone | custom fusion | bytes 7087104 | tf_op jit(solution)/shard_map/jit(take_along_axis)/gather | solution.py:228
  442.6 25.3 %gather_fusion.7 = bf16[1152,1536]{1,0:T(8,128)(2,1)} fusion(bf16[3,448,1536]{2,1,0:T(8,128)(2,1)} %bitcast.268, s32[1152]{0:T(1024)S(1)} %reshape.789), kind=kCustom, calls=%fused_computation.clone | custom fusion | bytes 7087104 | tf_op jit(solution)/shard_map/jit(take_along_axis)/gather | solution.py:228
  496.9 28.5 %gather_fusion.10 = bf16[1344,1536]{1,0:T(8,128)(2,1)} fusion(bf16[3,384,1536]{2,1,0:T(8,128)(2,1)S(1)} %add_convert_fusion, s32[1344]{0:T(1024)S(1)} %reshape.793), kind=kCustom, calls=%fused_computation.3.clone | custom fusion | bytes 8268288 | tf_op jit(solution)/shard_map/jit(take_along_axis)/gather | solution.py:232
  525.4 36.2 %gather_fusion.8 = bf16[1344,1536]{1,0:T(8,128)(2,1)} fusion(bf16[3,384,1536]{2,1,0:T(8,128)(2,1)} %convolution_convert_fusion.5, s32[1344]{0:T(1024)S(1)} %reshape.793), kind=kCustom, calls=%fused_computation.1.clone | custom fusion | bytes 8268288 | tf_op jit(solution)/shard_map/jit(take_along_axis)/gather | solution.py:232
  561.6 23.6 %fusion.32 = (bf16[3,448,1536]{2,0,1:T(4,128)(2,1)}, bf16[3,448,1536]{2,0,1:T(4,128)(2,1)S(1)}) fusion(bf16[3,448,1536]{2,1,0:T(8,128)(2,1)} %bitcast.287, pred[3,448]{0,1:T(8,128)(4,1)S(1)} %bitcast.317, pred[3,448]{0,1:T(8,128)(4,1)S(1)} %copy-done.42, bf16[3,448,1536]{2,1,0:T(8,128)(2,1)} %bitcast.288), kind=kLoop, calls=%fused_computation.67 | loop fusion | flops 8257536 | bytes 16517760 | tf_op jit(solution)/shard_map/jit(_where)/select_n | solution.py:233
  585.2 136.6 %all_to_all.77 = bf16[3,448,1536]{2,0,1:T(4,128)(2,1)} all-to-all(bf16[3,448,1536]{2,0,1:T(4,128)(2,1)S(1)} %get-tuple-element.487), channel_id=1, replica_groups=mesh['grp'=4,'ep'=8] {'ep'}, dimensions={1} | all-to-all | bytes 8257536 | tf_op jit(solution)/shard_map/all_to_all | solution.py:242
  721.8 8.0 all-to-all-start.4
  735.9 9.8 gather_fusion.3
  750.4 98.2 %all-to-all-done.4 = bf16[3,448,1536]{2,0,1:T(4,128)(2,1)} async-done(((bf16[3,448,1536]{2,0,1:T(4,128)(2,1)}), bf16[3,448,1536]{2,0,1:T(4,128)(2,1)}, u32[]{:S(2)}, u32[]{:S(2)}) %all-to-all-start.4) | async-done | bytes 4128800 | tf_op jit(solution)/shard_map/all_to_all | solution.py:268
  854.1 9.4 gather_fusion.5
  877.4 37.2 %while.29 = (s32[]{:T(128)}, f32[8,3,128,64]{2,3,1,0:T(8,128)}, f32[1024,1024]{0,1:T(8,128)}, bf16[128]{0:T(256)(128)(2,1)}, s32[2]{0:T(128)}, /*index=5*/bf16[1...) while((s32[]{:T(128)}, f32[8,3,128,64]{2,3,1,0:T(8,128)}, ...), condition=%wide.region_24.27_spmd.clone, body=%wide.region_23.26_spmd.clone.sunk | while | flops 1024590464 | bytes 45904428 | solution.py:352
  927.5 25.3 %reduce-scatter.19.cloned.1.call-done = bf16[128,1024]{1,0:T(8,128)(2,1)} async-done(((bf16[1024,1024]{1,0:T(8,128)(2,1)}), bf16[128,1024]{1,0:T(8,128)(2,1)}) %reduce-scatter.19.cloned.1.call-update) | async-done | bytes 262160
  968.9 11.0 copy.287
  995.2 10.9 copy.283
  1021.2 11.0 copy.285
  1039.2 58.6 %reduce-scatter.15.cloned.1.call-done = bf16[320,1536]{1,0:T(8,128)(2,1)} async-done(((bf16[2560,1536]{1,0:T(8,128)(2,1)}), bf16[320,1536]{1,0:T(8,128)(2,1)}) %reduce-scatter.15.cloned.1.call-update) | async-done | bytes 983056 | tf_op jit(solution)/shard_map/reduce_scatter | solution.py:381
  1099.0 53.3 %all-reduce.12.cloned.1.call-done = bf16[24,1536]{1,0:T(8,128)(2,1)} async-done(((bf16[24,1536]{1,0:T(8,128)(2,1)}), bf16[24,1536]{1,0:T(8,128)(2,1)}) %all-reduce.12.cloned.1.call-update) | async-done | bytes 73744
  1153.1 61.1 %reduce-scatter.25.cloned.1.call-done = bf16[384,1536]{1,0:T(8,128)(2,1)} async-done(((bf16[1536,1536]{1,0:T(8,128)(2,1)}), bf16[384,1536]{1,0:T(8,128)(2,1)}) %reduce-scatter.25.cloned.1.call-update) | async-done | bytes 1179664
  1221.9 52.2 %reduce-scatter.21.cloned.1.call-done = bf16[384,1536]{1,0:T(8,128)(2,1)} async-done(((bf16[1536,1536]{1,0:T(8,128)(2,1)}), bf16[384,1536]{1,0:T(8,128)(2,1)}) %reduce-scatter.21.cloned.1.call-update) | async-done | bytes 1179664
  1281.7 52.3 %reduce-scatter.23.cloned.1.call-done = bf16[384,1536]{1,0:T(8,128)(2,1)} async-done(((bf16[1536,1536]{1,0:T(8,128)(2,1)}), bf16[384,1536]{1,0:T(8,128)(2,1)}) %reduce-scatter.23.cloned.1.call-update) | async-done | bytes 1179664
  1346.9 10.7 all-reduce.5
  1357.8 15.4 %all-reduce.7 = (bf16[3,1536]{1,0:T(4,128)(2,1)S(1)}, bf16[192]{0:T(256)(128)(2,1)S(1)}, bf16[192]{0:T(256)(128)(2,1)S(1)}) all-reduce(bf16[3,1536]{1,0:T(4,128)(2,1)S(1)} %constant_dynamic-slice_fusion.4, bf16[192]{0:T(256)(128)(2,1)S(1)} %dynamic-slice.5, bf16[192]{0:T(256)(128)(2,1)S(1)} %dynamic-slice.7), channel_id=1, replica_groups=mesh['grp'=4,'ep'=8] {'grp'}, use_global_device_ids=true, to_apply=%region_32.35 | all-reduce | flops 4992 | bytes 19968 | tf_op jit(solution)/shard_map/psum | solution.py:400
  1375.9 22.1 %all-reduce.14.cloned.1.call-done = (bf16[320,1536]{1,0:T(8,128)(2,1)}, bf16[192,1536]{1,0:T(8,128)(2,1)}) async-done(((bf16[320,1536]{1,0:T(8,128)(2,1)}, bf16[192,1536]{1,0:T(8,128)(2,1)}), (bf16[320,1536]{1,0:T(8,128)(2,1)}, bf16[192,1536]{1,0:T(8,128)(2,1)})) %all-reduce.14.cloned.1.call-update) | async-done | bytes 1572880 | tf_op jit(solution)/shard_map/psum | solution.py:398
  (411 shorter events, 307.2 us)
Async XLA Ops:
  7.2 79.9 %all-gather.7.cloned.1.call-start = ((), (), s32[]{:S(2)}) async-start(), calls=%async_computation.11 | async-start | bytes 8847360 | tf_op jit(solution)/shard_map/all_gather | solution.py:87
  7.9 132.5 %all-gather.11.cloned.1.call-start = ((), (), s32[]{:S(2)}) async-start(), calls=%async_computation.13 | async-start | bytes 1179648 | tf_op jit(solution)/shard_map/all_gather | solution.py:146
  23.5 69.6 %copy-start.44 = (f32[1536]{0:T(1024)}, f32[1536]{0:T(1024)S(1)}, u32[]{:S(2)}) copy-start(f32[1536]{0:T(1024)S(1)} %convert_element_type.194) | copy-start | bytes 18436
  24.7 68.5 %copy-start.63 = (f32[128]{0:T(128)}, f32[128]{0:T(128)S(1)}, u32[]{:S(2)}) copy-start(f32[128]{0:T(128)S(1)} %add_rsqrt_fusion.1) | copy-start | bytes 1540
  24.7 70.9 %copy-start.50 = (s32[128,8]{0,1:T(8,128)S(1)}, s32[128,8]{0,1:T(8,128)}, u32[]{:S(2)}) copy-start(s32[128,8]{0,1:T(8,128)} %param.22) | copy-start | bytes 12292
  93.2 28.3 %copy-start.22 = (bf16[128,1536]{1,0:T(8,128)(2,1)S(1)}, bf16[128,1536]{1,0:T(8,128)(2,1)}, u32[]{:S(2)}) copy-start(bf16[128,1536]{1,0:T(8,128)(2,1)} %param.31) | copy-start | bytes 1179652
  93.2 34.6 %copy-start.73 = (s32[128]{0:T(128)S(1)}, s32[128]{0:T(128)}, u32[]{:S(2)}) copy-start(s32[128]{0:T(128)} %param.21) | copy-start | bytes 1540
  93.9 48.7 %all-gather.9.cloned.1.call-start = ((), (), s32[]{:S(2)}) async-start(), calls=%async_computation.12 | async-start | bytes 1179648 | tf_op jit(solution)/shard_map/all_gather | solution.py:145
  94.1 46.0 %copy-start.38 = (f32[128,32]{0,1:T(8,128)}, f32[128,32]{0,1:T(8,128)S(1)}, u32[]{:S(2)}) copy-start(f32[128,32]{0,1:T(8,128)S(1)} %get-tuple-element.494) | copy-start | bytes 49156
  94.1 46.0 %copy-start.40 = (f32[128,32]{0,1:T(8,128)}, f32[128,32]{0,1:T(8,128)S(1)}, u32[]{:S(2)}) copy-start(f32[128,32]{0,1:T(8,128)S(1)} %get-tuple-element.495) | copy-start | bytes 49156
  95.0 97.3 %all-gather.13.cloned.1.call-start = ((), (), s32[]{:S(2)}) async-start(), calls=%async_computation.14 | async-start | bytes 5308416 | tf_op jit(solution)/shard_map/all_gather | solution.py:88
  104.0 114.5 %all-to-all-start = ((bf16[8,3,2]{1,2,0:T(2,128)(2,1)}), bf16[8,3,2]{1,2,0:T(2,128)(2,1)S(1)}, u32[]{:S(2)}, u32[]{:S(2)}) async-start(bf16[8,3,2]{1,2,0:T(2,128)(2,1)} %copy.237), calls=%async_computation | async-start | bytes 8192 | tf_op jit(solution)/shard_map/all_to_all | solution.py:206
  109.3 87.2 %copy-start.48 = (f32[1536]{0:T(1024)}, f32[1536]{0:T(1024)S(1)}, u32[]{:S(2)}) copy-start(f32[1536]{0:T(1024)S(1)} %convert_element_type.201) | copy-start | bytes 18436
  121.5 75.9 %copy-start.34 = (bf16[24,1536]{1,0:T(8,128)(2,1)}, bf16[24,1536]{1,0:T(8,128)(2,1)S(1)}, u32[]{:S(2)}) copy-start(bf16[24,1536]{1,0:T(8,128)(2,1)S(1)} %reshape.778) | copy-start | bytes 221188
  142.7 49.7 %copy-start.9 = (bf16[128,1536]{1,0:T(8,128)(2,1)S(1)}, bf16[128,1536]{1,0:T(8,128)(2,1)}, u32[]{:S(2)}) copy-start(bf16[128,1536]{1,0:T(8,128)(2,1)} %param.20) | copy-start | bytes 1179652
  314.1 97.3 %all-to-all-start.1 = ((bf16[24,56,1536]{2,1,0:T(8,128)(2,1)}), bf16[24,56,1536]{2,1,0:T(8,128)(2,1)}, u32[]{:S(2)}, u32[]{:S(2)}) async-start(bf16[24,56,1536]{2,1,0:T(8,128)(2,1)} %get-tuple-element.493), calls=%async_computation.1 | async-start | bytes 8257536 | tf_op jit(solution)/shard_map/all_to_all | solution.py:205
  330.0 149.6 %copy-start.69 = (pred[3,384]{1,0:T(4,128)(4,1)}, pred[3,384]{1,0:T(4,128)(4,1)S(1)}, u32[]{:S(2)}) copy-start(pred[3,384]{1,0:T(4,128)(4,1)S(1)} %get-tuple-element.463) | copy-start | bytes 3460
  332.1 147.5 %copy-start.71 = (pred[3,384]{1,0:T(4,128)(4,1)}, pred[3,384]{1,0:T(4,128)(4,1)S(1)}, u32[]{:S(2)}) copy-start(pred[3,384]{1,0:T(4,128)(4,1)S(1)} %iota_compare_fusion.4) | copy-start | bytes 3460
  525.4 36.2 %copy-start.42 = (pred[3,448]{0,1:T(8,128)(4,1)S(1)}, pred[3,448]{0,1:T(8,128)(4,1)}, u32[]{:S(2)}) copy-start(pred[3,448]{0,1:T(8,128)(4,1)} %copy.244) | copy-start | bytes 4036
  525.4 36.2 %copy-start.43 = (pred[3,448,1]{0,1,2:T(8,128)(4,1)S(1)}, pred[3,448,1]{0,1,2:T(8,128)(4,1)}, u32[]{:S(2)}) copy-start(pred[3,448,1]{0,1,2:T(8,128)(4,1)} %copy.279) | copy-start | bytes 4036
  721.8 126.8 %all-to-all-start.4 = ((bf16[3,448,1536]{2,0,1:T(4,128)(2,1)}), bf16[3,448,1536]{2,0,1:T(4,128)(2,1)}, u32[]{:S(2)}, u32[]{:S(2)}) async-start(bf16[3,448,1536]{2,0,1:T(4,128)(2,1)} %get-tuple-element.486), calls=%async_computation.4 | async-start | bytes 11010048 | tf_op jit(solution)/shard_map/all_to_all | solution.py:268
  729.8 223.0 %reduce-scatter.19.cloned.1.call-start = ((), (), s32[]{:S(2)}) async-start(), calls=%async_computation.17 | async-start | bytes 2359296
  750.4 115.3 %copy-start.52 = (bf16[128,24]{0,1:T(8,128)(2,1)}, bf16[128,24]{0,1:T(8,128)(2,1)S(1)}, u32[]{:S(2)}) copy-start(bf16[128,24]{0,1:T(8,128)(2,1)S(1)} %select_reduce_fusion) | copy-start | bytes 18436
  922.5 116.7 %reduce-scatter.17.cloned.1.call-start = ((), (), s32[]{:S(2)}) async-start(), calls=%async_computation.16 | async-start | bytes 5308416 | tf_op jit(solution)/shard_map/reduce_scatter | solution.py:384
  926.2 27.9 %copy-start.45 = (f32[1536]{0:T(1024)S(1)}, f32[1536]{0:T(1024)}, u32[]{:S(2)}) copy-start(f32[1536]{0:T(1024)} %copy-done.44) | copy-start | bytes 18436
  926.2 27.9 %copy-start.64 = (f32[128]{0:T(128)S(1)}, f32[128]{0:T(128)}, u32[]{:S(2)}) copy-start(f32[128]{0:T(128)} %copy-done.63) | copy-start | bytes 1540
  926.2 171.5 %reduce-scatter.15.cloned.1.call-start = ((), (), s32[]{:S(2)}) async-start(), calls=%async_computation.15 | async-start | bytes 8847360 | tf_op jit(solution)/shard_map/reduce_scatter | solution.py:381
  959.6 192.7 %all-reduce.12.cloned.1.call-start = ((), (), s32[]{:S(2)}) async-start(), calls=%async_computation.21 | async-start | bytes 147456
  961.3 252.9 %reduce-scatter.25.cloned.1.call-start = ((), (), s32[]{:S(2)}) async-start(), calls=%async_computation.20 | async-start | bytes 5898240
  987.0 287.1 %reduce-scatter.21.cloned.1.call-start = ((), (), s32[]{:S(2)}) async-start(), calls=%async_computation.18 | async-start | bytes 5898240
  1013.1 321.0 %reduce-scatter.23.cloned.1.call-start = ((), (), s32[]{:S(2)}) async-start(), calls=%async_computation.19 | async-start | bytes 5898240
  1039.1 358.9 %all-reduce.14.cloned.1.call-start = ((), (), s32[]{:S(2)}) async-start(), calls=%async_computation.22 | async-start | bytes 3145728 | tf_op jit(solution)/shard_map/psum | solution.py:398
  (65 other events, 425.8 us)
Sparse Core Ops, SparseCore 0:
  9.6 77.4 all-gather.6
  94.0 22.0 all-gather.10
  118.3 22.5 all-gather.8
  142.3 49.9 all-gather.12
  922.6 30.0 reduce-scatter.18
  954.9 57.4 reduce-scatter.16
  1014.7 83.0 reduce-scatter.14
  1100.7 51.5 all-reduce.11
  1155.3 58.8 reduce-scatter.24
  1217.0 56.9 reduce-scatter.20
  1277.1 56.9 reduce-scatter.22
  1337.0 60.9 all-reduce.13
where the time goes:
time: 1420 us; the launch traced here: 1410 us
  waiting for transfers between devices  582 us (41%)
  blocking collectives  293 us (21%)
  local copies, waits for them, and re-layouts  288 us (20%)
  matrix products  111 us (8%)
  other arithmetic  92.9 us (7%)
  starting transfers between devices  22.2 us (2%)
  between operations  17.9 us (1%)
    unnamed x17, waiting for transfers between devices  246 us
    all_to_all x1, blocking collectives, local(): lax.all_to_all(spread(expert_out), 'ep', split_axis=1, concat_axis=0, til...  137 us
    all_to_all x1, waiting for transfers between devices, local(): lax.all_to_all(spread(slot_grad), 'ep', split_axis=1, concat_axis=0, tile...  98.2 us
    all_to_all x1, blocking collectives, local(): lax.all_to_all(outgoing_grad, 'ep', split_axis=0, concat_axis=1, tiled=True)  95.6 us
    unnamed x178, local copies, waits for them, and re-layouts  86.1 us
    all_to_all x1, waiting for transfers between devices, local(): lax.all_to_all(outgoing, 'ep', split_axis=0, concat_axis=1, tiled=True)  74.8 us
    gather x3, local copies, waits for them, and re-layouts, spread(): taken = jnp.take_along_axis(rows, slot_pick[:, :, None], axis=1)  64.8 us
    all_gather x1, waiting for transfers between devices, local(): lax.all_gather(qkv_weight, 'ep', axis=0, tiled=True)  62.4 us
  transfers between devices with their start and end apart: 15, of which 11 were waited for; matrix products, arithmetic and copies ran while one was open for 16% of the time, Pallas kernels for 0%

commit v1 on v0

v1 whole, which is shorter than its diff:
```python
import jax
import jax.numpy as jnp
from jax import lax
from jax.sharding import PartitionSpec as P

QUERY_HEADS = 24
KEY_VALUE_HEADS = 8
HEAD_DIMENSION = 64
TOPK = 8

eps = 1e-06
theta = 10000.0
negative_large = -1e30
f32 = jnp.float32
bf16 = jnp.bfloat16


def angles(token_positions, head_size):
    half = head_size // 2
    freq = theta ** (-jnp.arange(half, dtype=f32) * 2.0 / head_size)
    angle = token_positions.astype(f32)[:, None] * freq[None, :]
    return (jnp.cos(angle)[:, None, :], jnp.sin(angle)[:, None, :])


def rotate(value_matrix, cosine_table, sine_table):
    half = value_matrix.shape[-1] // 2
    first = value_matrix[..., :half]
    second = value_matrix[..., half:]
    return jnp.concatenate(
        [
            first * cosine_table - second * sine_table,
            second * cosine_table + first * sine_table,
        ],
        axis=-1,
    )


def norm_back(delta, normed, scale, gain):
    scaled = delta * gain
    return scale * (scaled - normed * jnp.mean(scaled * normed, axis=-1, keepdims=True))


def head_plan(devices):
    per_query = QUERY_HEADS // devices
    per_key = KEY_VALUE_HEADS // devices
    blocks = QUERY_HEADS + 2 * KEY_VALUE_HEADS
    own = blocks // devices

    def place(block):
        if block < QUERY_HEADS:
            return block // per_query, block % per_query
        block -= QUERY_HEADS
        if block < KEY_VALUE_HEADS:
            return block // per_key, per_query + block % per_key
        block -= KEY_VALUE_HEADS
        return block // per_key, per_query + per_key + block % per_key

    left = [[(s, *place(i * own + s)) for s in range(own)] for i in range(devices)]
    rounds = []
    for _ in range(own):
        taken = {}

        def assign(i, seen):
            for edge in left[i]:
                j = edge[1]
                if j in seen:
                    continue
                seen.add(j)
                if j not in taken or assign(taken[j][0], seen):
                    taken[j] = (i, edge)
                    return True
            return False

        for i in range(devices):
            assign(i, set())
        source_slot, target, target_slot = [0] * devices, [0] * devices, [0] * devices
        for j, (i, edge) in taken.items():
            source_slot[i], target[i], target_slot[j] = edge[0], j, edge[2]
            left[i].remove(edge)
        rounds.append((source_slot, target, target_slot))
    return rounds


def move_blocks(blocks, pick, pairs, order):
    got = [
        lax.ppermute(lax.dynamic_index_in_dim(blocks, slot, 0, keepdims=False), "ep", pair)
        for slot, pair in zip(pick, pairs)
    ]
    return jnp.stack(got)[order]


def local(
    layer_in,
    segments,
    routes,
    qkv_weight,
    out_weight,
    router_weight,
    norm1_gain,
    norm2_gain,
    w_gate,
    w_up,
    w_down,
    out_cotangent,
):
    tokens, width = layer_in.shape
    devices = lax.axis_size("ep")
    me = lax.axis_index("ep")
    copies = lax.axis_size("grp")
    mine = w_gate.shape[0]
    hidden = w_gate.shape[1]
    experts = mine * devices
    seq = tokens * devices
    capacity = 9 * tokens * TOPK // (8 * mine)
    heads = QUERY_HEADS // devices
    keys = KEY_VALUE_HEADS // devices
    group = heads // keys
    hd = HEAD_DIMENSION
    scale = hd ** (-0.5)

    x_all = lax.all_gather(layer_in, "ep", axis=0, tiled=True)
    gain_width = norm1_gain.shape[0]
    small = jnp.concatenate(
        [
            router_weight.reshape(-1),
            norm1_gain,
            norm2_gain,
            routes.T.astype(bf16).reshape(-1),
            segments.astype(bf16),
        ]
    )
    small_all = lax.all_gather(small, "ep", axis=0, tiled=False)
    cut = mine * width
    full_router = small_all[:, :cut].reshape(experts, width)
    gain_one = small_all[:, cut : cut + gain_width].reshape(1, width).astype(f32)
    gain_two = small_all[:, cut + gain_width : cut + 2 * gain_width].reshape(1, width).astype(f32)
    cut += 2 * gain_width
    routes_all = small_all[:, cut : cut + tokens * TOPK].reshape(devices, TOPK, tokens)
    routes_all = routes_all.transpose(1, 0, 2).reshape(TOPK, seq).astype(jnp.int32)
    seg_all = small_all[:, cut + tokens * TOPK :].reshape(seq)

    rounds = head_plan(devices)
    slots = len(rounds)
    to_heads = [[(i, t[i]) for i in range(devices)] for _, t, _ in rounds]
    to_rows = [[(b, a) for a, b in pair] for pair in to_heads]
    pick_row = [jnp.array(s, jnp.int32)[me] for s, _, _ in rounds]
    pick_head = [jnp.array(s, jnp.int32)[me] for _, _, s in rounds]
    order_head = jnp.array(
        [[[r[2][d] for r in rounds].index(s) for s in range(slots)] for d in range(devices)],
        jnp.int32,
    )[me]
    order_row = jnp.array(
        [[[r[0][d] for r in rounds].index(s) for s in range(slots)] for d in range(devices)],
        jnp.int32,
    )[me]
    block_rows = qkv_weight.shape[0] // slots
    qkv_heads = move_blocks(
        qkv_weight.reshape(slots, block_rows, width), pick_row, to_heads, order_head
    ).reshape(slots * block_rows, width)
    full_out = lax.all_gather(out_weight, "ep", axis=0, tiled=True)

    expert_row = jnp.arange(experts, dtype=jnp.int32)[:, None, None]
    chosen = jnp.any(routes_all[None] == expert_row, axis=1)
    own_chosen = lax.dynamic_slice_in_dim(chosen, me * mine, mine, 0)
    before = (
        jnp.arange(seq, dtype=jnp.int32)[:, None] < jnp.arange(seq, dtype=jnp.int32)[None, :]
    ).astype(bf16)
    rank = jnp.einsum(
        "es,st->et", own_chosen.astype(bf16), before, preferred_element_type=f32
    ).astype(jnp.int32)
    rank = jnp.where(own_chosen, rank, -1)
    places = jnp.arange(capacity, dtype=jnp.int32)[None, :, None]
    pick = rank[:, None, :] == places
    pick_low = pick.astype(bf16).reshape(mine * capacity, seq)

    residual_all = x_all.astype(f32)
    scale_one_all = lax.rsqrt(jnp.mean(residual_all * residual_all, axis=-1, keepdims=True) + eps)
    normed_all = residual_all * scale_one_all
    x_low = (normed_all * gain_one).astype(bf16)
    projected = jnp.einsum("td,cd->tc", x_low, qkv_heads, preferred_element_type=f32)
    positions = jnp.arange(seq, dtype=jnp.int32)
    cosine_table, sine_table = angles(positions, hd)
    turned = rotate(
        projected[:, : (heads + keys) * hd].reshape(seq, heads + keys, hd),
        cosine_table,
        sine_table,
    ).astype(bf16)
    query = turned[:, :heads].reshape(seq, keys, group, hd).transpose(1, 2, 0, 3)
    key = turned[:, heads:].transpose(1, 0, 2)
    value = (
        projected[:, (heads + keys) * hd :].astype(bf16).reshape(seq, keys, hd).transpose(1, 0, 2)
    )
    valid = (seg_all[:, None] == seg_all[None, :]) & (positions[None, :] <= positions[:, None])
    score = jnp.einsum("hgqd,hkd->hgqk", query, key, preferred_element_type=f32) * scale
    score = jnp.where(valid, score, negative_large)
    top = jnp.max(score, axis=-1, keepdims=True)
    weight = jnp.where(valid, jnp.exp(score - top), 0.0)
    prob = weight / jnp.sum(weight, axis=-1, keepdims=True)
    prob_low = prob.astype(bf16)
    attended = jnp.einsum("hgqk,hkd->hgqd", prob_low, value, preferred_element_type=f32)
    mixed_heads = attended.transpose(2, 0, 1, 3).reshape(seq, heads * hd).astype(bf16)
    mixed = lax.all_to_all(mixed_heads, "ep", split_axis=0, concat_axis=1, tiled=True)

    branch = jnp.einsum("tc,dc->td", mixed, full_out, preferred_element_type=f32)
    hidden_one = layer_in.astype(f32) + branch
    scale_two = lax.rsqrt(jnp.mean(hidden_one * hidden_one, axis=-1, keepdims=True) + eps)
    normed_two = hidden_one * scale_two
    x_two = (normed_two * gain_two).astype(bf16)
    x_two_all = lax.all_gather(x_two, "ep", axis=0, tiled=True)
    late_cotangent, late_mixed, _ = lax.optimization_barrier((out_cotangent, mixed, x_two))
    g_all = lax.all_gather(late_cotangent, "ep", axis=0, tiled=True)
    mixed_all = lax.all_gather(late_mixed, "ep", axis=0, tiled=True)

    logits = jnp.einsum("ed,td->et", full_router, x_two_all, preferred_element_type=f32)
    logits = jnp.where(chosen, logits, negative_large)
    raised = jnp.where(chosen, jnp.exp(logits - jnp.max(logits, axis=0, keepdims=True)), 0.0)
    gates = raised / jnp.sum(raised, axis=0, keepdims=True)
    own_gates = lax.dynamic_slice_in_dim(gates, me * mine, mine, 0)
    place_gate = jnp.sum(jnp.where(pick, own_gates[:, None, :], 0.0), axis=-1)[:, :, None]

    def gather(rows):
        picked = jnp.einsum("pt,td->pd", pick_low, rows, preferred_element_type=f32)
        return picked.astype(bf16).reshape(mine, capacity, width)

    def scatter(rows):
        back = jnp.einsum(
            "pt,pd->td", pick_low, rows.reshape(mine * capacity, width), preferred_element_type=f32
        )
        return back.astype(bf16)

    def shares(left, right):
        grad = jnp.einsum("jcf,jcd->jfd", left, right, preferred_element_type=f32).astype(bf16)
        grad = grad.reshape(mine * hidden, copies, width // copies).transpose(1, 0, 2)
        return grad.reshape(copies * mine * hidden, width // copies)

    def grp_sum(part):
        total = lax.psum_scatter(part, "grp", scatter_dimension=0, tiled=True)
        return total.astype(f32).reshape(mine, hidden, width // copies)

    dense_in = gather(x_two_all)
    dense_g = gather(g_all)
    gate_pre = jnp.einsum("jcd,jfd->jcf", dense_in, w_gate, preferred_element_type=f32)
    up_pre = jnp.einsum("jcd,jfd->jcf", dense_in, w_up, preferred_element_type=f32)
    logistic = jax.nn.sigmoid(gate_pre)
    inner = (gate_pre * logistic * up_pre).astype(bf16)
    expert_out = jnp.einsum("jcf,jfd->jcd", inner, w_down, preferred_element_type=f32)
    place_dgate = jnp.sum(expert_out * dense_g.astype(f32), axis=-1)
    dgate_own = jnp.sum(jnp.where(pick, place_dgate[:, :, None], 0.0), axis=1)
    out_part = scatter((place_gate * expert_out).astype(bf16))
    dense_grad = (place_gate * dense_g.astype(f32)).astype(bf16)
    inner_grad = jnp.einsum("jcd,jfd->jcf", dense_grad, w_down, preferred_element_type=f32)
    gate_back = (inner_grad * up_pre * logistic * (1.0 + gate_pre * (1.0 - logistic))).astype(bf16)
    up_back = (inner_grad * gate_pre * logistic).astype(bf16)
    slot_grad = jnp.einsum(
        "jcf,jfd->jcd", gate_back, w_gate, preferred_element_type=f32
    ) + jnp.einsum("jcf,jfd->jcd", up_back, w_up, preferred_element_type=f32)
    back_part = scatter(slot_grad.astype(bf16))
    two_grad = lax.psum_scatter(back_part, "ep", scatter_dimension=0, tiled=True).astype(f32)
    dgate = lax.all_to_all(dgate_own, "ep", split_axis=1, concat_axis=0, tiled=True)
    down_part = shares(inner, dense_grad)
    gate_part = shares(gate_back, dense_in)
    up_part = shares(up_back, dense_in)

    delta = out_cotangent.astype(f32)
    gates_here = lax.dynamic_slice_in_dim(gates, me * tokens, tokens, 1)
    chosen_grad = gates_here * (dgate - jnp.sum(gates_here * dgate, axis=0, keepdims=True))
    logit_grad = chosen_grad.astype(bf16)
    router_grad = jnp.einsum("et,td->ed", logit_grad, x_two, preferred_element_type=f32)
    two_grad = two_grad + jnp.einsum(
        "et,ed->td", logit_grad, full_router, preferred_element_type=f32
    )
    gain_two_grad = jnp.sum(two_grad * normed_two, axis=0, keepdims=True)
    hidden_grad = delta + norm_back(two_grad, normed_two, scale_two, gain_two)
    hidden_low = hidden_grad.astype(bf16)
    mixing = jnp.einsum("td,dc->tc", hidden_low, full_out, preferred_element_type=f32)
    mixing_heads = lax.all_to_all(
        mixing.astype(bf16), "ep", split_axis=1, concat_axis=0, tiled=True
    )
    hidden_cols = lax.all_to_all(hidden_low, "ep", split_axis=1, concat_axis=0, tiled=True)

    change = mixing_heads.reshape(seq, keys, group, hd).transpose(1, 2, 0, 3)
    prob_grad = jnp.einsum("hgqd,hkd->hgqk", change, value, preferred_element_type=f32)
    row = jnp.sum(prob * prob_grad, axis=-1, keepdims=True)
    score_grad = (prob * (prob_grad - row)).astype(bf16)
    value_grad = jnp.einsum("hgqk,hgqd->hkd", prob_low, change, preferred_element_type=f32)
    query_grad = jnp.einsum("hgqk,hkd->hgqd", score_grad, key, preferred_element_type=f32) * scale
    key_grad = jnp.einsum("hgqk,hgqd->hkd", score_grad, query, preferred_element_type=f32) * scale
    turned_grad = jnp.concatenate(
        [
            query_grad.transpose(2, 0, 1, 3).reshape(seq, heads, hd),
            key_grad.transpose(1, 0, 2),
        ],
        axis=1,
    )
    turned_grad = rotate(turned_grad, cosine_table, -sine_table).reshape(seq, (heads + keys) * hd)
    proj_grad = jnp.concatenate(
        [turned_grad, value_grad.transpose(1, 0, 2).reshape(seq, keys * hd)], axis=1
    ).astype(bf16)
    one_part = jnp.einsum("tc,cd->td", proj_grad, qkv_heads, preferred_element_type=f32)
    gain_one_grad = jnp.sum(one_part * normed_all, axis=0, keepdims=True)
    one_grad = lax.psum_scatter(
        one_part.astype(bf16), "ep", scatter_dimension=0, tiled=True
    ).astype(f32)
    qkv_grad = jnp.einsum("tc,td->cd", proj_grad, x_low, preferred_element_type=f32)
    out_grad = jnp.einsum("td,tc->dc", hidden_cols, mixed_all, preferred_element_type=f32)

    small_sum = lax.psum(
        jnp.concatenate([router_grad, gain_one_grad, gain_two_grad], axis=0), ("grp", "ep")
    )
    router_sum = lax.dynamic_slice_in_dim(small_sum[:experts], me * mine, mine, 0)
    gain_sums = lax.dynamic_slice_in_dim(small_sum[experts:], me * gain_width, gain_width, 1)
    qkv_sum = lax.psum(qkv_grad.astype(bf16), "grp")
    qkv_rows = move_blocks(
        qkv_sum.reshape(slots, block_rows, width), pick_head, to_rows, order_row
    ).reshape(slots * block_rows, width)
    out_sum = lax.psum(out_grad.astype(bf16), "grp")

    returned = lax.psum_scatter(out_part, "ep", scatter_dimension=0, tiled=True)
    layer_out = (hidden_one + returned.astype(f32)).astype(bf16)
    residual = layer_in.astype(f32)
    scale_one = lax.rsqrt(jnp.mean(residual * residual, axis=-1, keepdims=True) + eps)
    grad_in = (hidden_grad + norm_back(one_grad, residual * scale_one, scale_one, gain_one)).astype(
        bf16
    )
    return (
        layer_out,
        grad_in,
        qkv_rows.astype(f32),
        out_sum.astype(f32),
        router_sum,
        gain_sums[0],
        gain_sums[1],
        grp_sum(gate_part),
        grp_sum(up_part),
        grp_sum(down_part),
    )


def solution(mesh):
    in_specs = (
        P(("grp", "ep"), None),
        P(("grp", "ep")),
        P(("grp", "ep"), None),
        P("ep", None),
        P("ep", None),
        P("ep", None),
        P("ep"),
        P("ep"),
        P("ep", None, None),
        P("ep", None, None),
        P("ep", None, None),
        P(("grp", "ep"), None),
    )
    out_specs = (
        P(("grp", "ep"), None),
        P(("grp", "ep"), None),
        P("ep", None),
        P("ep", None),
        P("ep", None),
        P("ep"),
        P("ep"),
        P("ep", None, "grp"),
        P("ep", None, "grp"),
        P("ep", None, "grp"),
    )
    return jax.shard_map(local, mesh=mesh, in_specs=in_specs, out_specs=out_specs, check_vma=False)
```

time: 1420 us -> 829 us (0.58)
  blocking collectives: 293 us -> 24.4 us
  local copies, waits for them, and re-layouts: 288 us -> 83.2 us
  waiting for transfers between devices: 582 us -> 448 us
  other arithmetic: 92.9 us -> 42.1 us
  starting transfers between devices: 22.2 us -> 50.1 us
  matrix products: 111 us -> 134 us
  between operations: 17.9 us -> 33 us
    unnamed x17 -> x13, waiting for transfers between devices: 246 us -> 2.43 us
    all_to_all x2 -> x0, blocking collectives: 232 us -> none  [the longest x1 137 us: local(): lax.all_to_all(spread(expert_out), 'ep', split_axis=1, concat_axis=0, til...]
    reduce_scatter x2 -> x6, waiting for transfers between devices: 58.6 us -> 253 us  [the longest x3 150 us: grp_sum(): total = lax.psum_scatter(part, 'grp', scatter_dimension=0, tiled=True)]
    gather x17 -> x2, local copies, waits for them, and re-layouts: 156 us -> 1.22 us  [move_blocks(): return jnp.stack(got)[order]]
    all_to_all x3 -> x4, waiting for transfers between devices: 173 us -> 23.8 us  [the longest x1 16.8 us: local(): lax.all_to_all(mixed_heads, 'ep', split_axis=0, concat_axis=1, tiled=True)]
    psum x1 -> x2, waiting for transfers between devices: 22.1 us -> 104 us  [the longest x1 62.7 us: local(): qkv_sum = lax.psum(qkv_grad.astype(bf16), 'grp')]
    unnamed x178 -> x138, local copies, waits for them, and re-layouts: 86.1 us -> 9.86 us
    reshape x0 -> x9, local copies, waits for them, and re-layouts: none -> 45.3 us  [the longest x6 42.6 us: shares(): grad.reshape(mine * hidden, copies, width // copies).transpose(1, 0, 2)]
  transfers between devices with their start and end apart: 15 -> 27, of which waited for: 11 -> 15; matrix products, arithmetic and copies ran while one was open for 16% -> 24% of each run, Pallas kernels for 0% -> 0%
where the time goes in v1:
time: 829 us; the launch traced here: 814 us
  waiting for transfers between devices  448 us (54%)
  matrix products  134 us (16%)
  local copies, waits for them, and re-layouts  83.2 us (10%)
  starting transfers between devices  50.1 us (6%)
  other arithmetic  42.1 us (5%)
  between operations  33 us (4%)
  blocking collectives  24.4 us (3%)
    reduce_scatter x3, waiting for transfers between devices, grp_sum(): total = lax.psum_scatter(part, 'grp', scatter_dimension=0, tiled=True)  150 us
    psum x1, waiting for transfers between devices, local(): qkv_sum = lax.psum(qkv_grad.astype(bf16), 'grp')  62.7 us
    reshape x6, local copies, waits for them, and re-layouts, shares(): grad.reshape(mine * hidden, copies, width // copies).transpose(1, 0, 2)  42.6 us
    psum x1, waiting for transfers between devices, local(): lax.psum(jnp.concatenate([router_grad, gain_one_grad, gain_two_grad], axi...  41.7 us
    reduce_scatter x1, waiting for transfers between devices, local(): returned = lax.psum_scatter(out_part, 'ep', scatter_dimension=0, tiled=True)  40.7 us
    reduce_scatter x1, waiting for transfers between devices, local(): lax.psum_scatter(one_part.astype(bf16), 'ep', scatter_dimension=0, tiled=...  36.7 us
    all_gather x1, waiting for transfers between devices, local(): x_two_all = lax.all_gather(x_two, 'ep', axis=0, tiled=True)  35.6 us
    reduce_scatter x1, waiting for transfers between devices, local(): lax.psum_scatter(back_part, 'ep', scatter_dimension=0, tiled=True)  25 us
  transfers between devices with their start and end apart: 27, of which 15 were waited for; matrix products, arithmetic and copies ran while one was open for 24% of the time, Pallas kernels for 0%

profile of v1, /device:TPU:16, one launch (start us, length us, event | category | flops | bytes accessed | tf_op | source)
XLA Modules:
  0.0 813.9 jit_solution(11952017074831056703)
XLA Ops:
  38.6 24.4 %all-gather = bf16[49152]{0:T(1024)(128)(2,1)S(1)} all-gather(bf16[6144]{0:T(1024)(128)(2,1)S(1)} %concatenate.21), channel_id=2, replica_groups=mesh['grp'=4,'ep'=8] {'ep'}, dimensions={0}, use_global_device_ids=true | all-gather | bytes 110592 | tf_op jit(solution)/shard_map/all_gather | solution.py:132
  77.5 8.1 fusion.87
  85.7 6.0 fusion.29
  92.6 6.3 all-to-all-start
  99.0 16.8 %all-to-all-done = bf16[8,128,192]{1,2,0:T(8,128)(2,1)S(1)} async-done(((bf16[8,128,192]{1,2,0:T(8,128)(2,1)}), bf16[8,128,192]{1,2,0:T(8,128)(2,1)S(1)}, u32[]{:S(2)}, u32[]{:S(2)}) %all-to-all-start) | async-done | bytes 393248 | tf_op jit(solution)/shard_map/all_to_all | solution.py:202
  126.0 35.6 %all-gather.11.cloned.1.call-done = bf16[1024,1536]{1,0:T(8,128)(2,1)} async-done(((bf16[128,1536]{1,0:T(8,128)(2,1)}), bf16[1024,1536]{1,0:T(8,128)(2,1)}) %all-gather.11.cloned.1.call-update) | async-done | bytes 3145744 | tf_op jit(solution)/shard_map/all_gather | solution.py:209
  166.0 6.2 convolution_convert_fusion.1
  179.5 20.8 %all-gather.13.cloned.1.call-done = bf16[1024,1536]{1,0:T(8,128)(2,1)} async-done(((bf16[128,1536]{1,0:T(8,128)(2,1)}), bf16[1024,1536]{1,0:T(8,128)(2,1)}) %all-gather.13.cloned.1.call-update) | async-done | bytes 3145744 | tf_op jit(solution)/shard_map/all_gather | solution.py:211
  200.3 6.2 convolution_convert_fusion
  206.5 9.0 %fusion.5 = (f32[3,384]{1,0:T(4,128)S(1)}, f32[3,384,1536]{2,1,0:T(8,128)}) fusion(bf16[3,384,1536]{2,1,0:T(8,128)(2,1)S(1)} %bitcast.239, bf16[3,384,512]{2,1,0:T(8,128)(2,1)S(1)} %copy-done.18, bf16[3,512,1536]{2,1,0:T(8,128)(2,1)} %param.34), kind=kOutput, calls=%fused_computation.17 | convolution fusion | flops 1817246592 | bytes 16519680 | tf_op jit(solution)/shard_map/jcf,jfd->jcd/dot_general | solution.py:246
  217.4 6.2 multiply_convert_fusion.3
  228.6 10.6 %bitcast_convert_fusion = bf16[1024,1536]{1,0:T(8,128)(2,1)} fusion(s32[3,1024]{1,0:T(4,128)} %copy-done.30, f32[3,384,1536]{2,1,0:T(8,128)} %fusion.94, bf16[3,384,512]{2,1,0:T(8,128)(2,1)} %get-tuple-element.22, bf16[3,512,1536]{2,1,0:T(8,128)(2,1)} %param.33), kind=kOutput, calls=%fused_computation.23 | convolution fusion | flops 5442109440 | bytes 16134144 | tf_op jit(solution)/shard_map/pt,pd->td/dot_general | solution.py:226
  251.5 25.0 %reduce-scatter.9.cloned.1.call-done = bf16[128,1536]{1,0:T(8,128)(2,1)} async-done(((bf16[1024,1536]{1,0:T(8,128)(2,1)}), bf16[128,1536]{1,0:T(8,128)(2,1)}) %reduce-scatter.9.cloned.1.call-update) | async-done | bytes 393232 | tf_op jit(solution)/shard_map/reduce_scatter | solution.py:258
  287.7 8.1 all-to-all-start.2
  305.1 7.4 all-to-all-start.3
  316.5 6.7 multiply_reduce_fusion
  323.3 8.3 %multiply_convert_fusion = bf16[3,1024,1024]{1,2,0:T(8,128)(2,1)S(1)} fusion(f32[3,1024,1024]{1,2,0:T(8,128)S(1)} %get-tuple-element.58, f32[3,1024]{1,0:T(4,128)S(1)} %get-tuple-element.57, f32[3,1024,1024]{1,2,0:T(8,128)} %get-tuple-element.47, f32[3,1024]{1,0:T(4,128)S(1)} %copy-done.36), kind=kLoop, calls=%fused_computation.3 | loop fusion | flops 12582912 | bytes 31481856 | tf_op jit(solution)/shard_map/convert_element_type | solution.py:284
  351.0 7.2 convolution_convert_fusion.2
  358.2 9.1 %reshape.415 = bf16[1536,4,384]{2,1,0:T(4,128)(2,1)} reshape(bf16[3,512,1536]{2,1,0:T(8,128)(2,1)} %convolution_convert_fusion.2) | data formatting | bytes 9437184 | tf_op jit(solution)/shard_map/reshape | solution.py:233
  372.5 5.7 convolution_convert_fusion.3
  378.2 9.1 %reshape.411 = bf16[1536,4,384]{2,1,0:T(4,128)(2,1)} reshape(bf16[3,512,1536]{2,1,0:T(8,128)(2,1)} %convolution_convert_fusion.3) | data formatting | bytes 9437184 | tf_op jit(solution)/shard_map/reshape | solution.py:233
  392.5 5.7 convolution_convert_fusion.4
  398.1 9.1 %reshape.407 = bf16[1536,4,384]{2,1,0:T(4,128)(2,1)} reshape(bf16[3,512,1536]{2,1,0:T(8,128)(2,1)} %convolution_convert_fusion.4) | data formatting | bytes 9437184 | tf_op jit(solution)/shard_map/reshape | solution.py:233
  413.3 9.0 %bitcast_convert_fusion.1 = bf16[1024,1536]{1,0:T(8,128)(2,1)} fusion(f32[3,384,1536]{2,1,0:T(8,128)} %get-tuple-element.53, f32[3,384]{1,0:T(4,128)S(1)} %copy-done.40, s32[3,1024]{1,0:T(4,128)S(1)} %copy-done.32), kind=kOutput, calls=%fused_computation.24 | convolution fusion | flops 3630170112 | bytes 10240512 | tf_op jit(solution)/shard_map/pt,pd->td/dot_general | solution.py:226
  436.5 41.7 %all-reduce.4.cloned.1.call-done = f32[26,1536]{1,0:T(8,128)} async-done(((f32[26,1536]{1,0:T(8,128)}), f32[26,1536]{1,0:T(8,128)}) %all-reduce.4.cloned.1.call-update) | async-done | bytes 159760 | tf_op jit(solution)/shard_map/psum | solution.py:307
  480.5 62.7 %all-reduce.6.cloned.1.call-done = (bf16[5,64,1536]{2,1,0:T(8,128)(2,1)}, bf16[192,1536]{1,0:T(8,128)(2,1)}) async-done(((bf16[5,64,1536]{2,1,0:T(8,128)(2,1)}, bf16[192,1536]{1,0:T(8,128)(2,1)}), (bf16[5,64,1536]{2,1,0:T(8,128)(2,1)}, bf16[192,1536]{1,0:T(8,128)(2,1)})) %all-reduce.6.cloned.1.call-update) | async-done | bytes 1572880 | tf_op jit(solution)/shard_map/psum | solution.py:312
  557.6 6.8 collective-permute-done.6
  566.7 36.4 %reduce-scatter.17.cloned.1.call-done = bf16[1536,384]{1,0:T(8,128)(2,1)} async-done(((bf16[6144,384]{1,0:T(8,128)(2,1)}), bf16[1536,384]{1,0:T(8,128)(2,1)}) %reduce-scatter.17.cloned.1.call-update) | async-done | bytes 1179664 | tf_op jit(solution)/shard_map/reduce_scatter | solution.py:237
  606.0 57.0 %reduce-scatter.15.cloned.1.call-done = bf16[1536,384]{1,0:T(8,128)(2,1)} async-done(((bf16[6144,384]{1,0:T(8,128)(2,1)}), bf16[1536,384]{1,0:T(8,128)(2,1)}) %reduce-scatter.15.cloned.1.call-update) | async-done | bytes 1179664 | tf_op jit(solution)/shard_map/reduce_scatter | solution.py:237
  666.0 57.0 %reduce-scatter.13.cloned.1.call-done = bf16[1536,384]{1,0:T(8,128)(2,1)} async-done(((bf16[6144,384]{1,0:T(8,128)(2,1)}), bf16[1536,384]{1,0:T(8,128)(2,1)}) %reduce-scatter.13.cloned.1.call-update) | async-done | bytes 1179664 | tf_op jit(solution)/shard_map/reduce_scatter | solution.py:237
  725.8 36.7 %reduce-scatter.11.cloned.1.call-done = bf16[128,1536]{1,0:T(8,128)(2,1)} async-done(((bf16[1024,1536]{1,0:T(8,128)(2,1)}), bf16[128,1536]{1,0:T(8,128)(2,1)}) %reduce-scatter.11.cloned.1.call-update) | async-done | bytes 393232 | tf_op jit(solution)/shard_map/reduce_scatter | solution.py:301
  763.8 40.7 %reduce-scatter.7.cloned.1.call-done = bf16[128,1536]{1,0:T(8,128)(2,1)} async-done(((bf16[1024,1536]{1,0:T(8,128)(2,1)}), bf16[128,1536]{1,0:T(8,128)(2,1)}) %reduce-scatter.7.cloned.1.call-update) | async-done | bytes 393232 | tf_op jit(solution)/shard_map/reduce_scatter | solution.py:318
  (293 shorter events, 175.6 us)
Async XLA Ops:
  7.2 63.1 %all-gather.7.cloned.1.call-start = ((), (), s32[]{:S(2)}) async-start(), calls=%async_computation.10 | async-start | bytes 3538944 | tf_op jit(solution)/shard_map/all_gather | solution.py:121
  7.9 108.9 %all-gather.9.cloned.1.call-start = ((), (), s32[]{:S(2)}) async-start(), calls=%async_computation.11 | async-start | bytes 5308416 | tf_op jit(solution)/shard_map/all_gather | solution.py:160
  9.6 60.1 %collective-permute-start.4 = (bf16[64,1536]{1,0:T(8,128)(2,1)}, bf16[64,1536]{1,0:T(8,128)(2,1)S(1)}, u32[]{:S(2)}, u32[]{:S(2)}) collective-permute-start(bf16[64,1536]{1,0:T(8,128)(2,1)} %slice.70), channel_id=1, source_target_pairs={{0,1},{1,3},{2,4},{3,6},{4,0},{5,5},{6,2},{7,7},{8,9},{9,11},{10,1... | collective-permute-start | bytes 589832 | tf_op jit(solution)/shard_map/ppermute | solution.py:86
  25.6 43.1 %collective-permute-start.3 = (bf16[64,1536]{1,0:T(8,128)(2,1)S(1)}, bf16[64,1536]{1,0:T(8,128)(2,1)}, u32[]{:S(2)}, u32[]{:S(2)}) collective-permute-start(bf16[64,1536]{1,0:T(8,128)(2,1)S(1)} %get-tuple-element.33), channel_id=1, source_target_pairs={{0,0},{1,2},{2,3},{3,5},{4,7},{5,4},{6,1},{7,6},{8,8},{9,10},{10,1... | collective-permute-start | bytes 589832 | tf_op jit(solution)/shard_map/ppermute | solution.py:86
  28.1 39.6 %collective-permute-start.2 = (bf16[64,1536]{1,0:T(8,128)(2,1)S(1)}, bf16[64,1536]{1,0:T(8,128)(2,1)}, u32[]{:S(2)}, u32[]{:S(2)}) collective-permute-start(bf16[64,1536]{1,0:T(8,128)(2,1)S(1)} %get-tuple-element.34), channel_id=1, source_target_pairs={{0,1},{1,2},{2,4},{3,6},{4,7},{5,3},{6,0},{7,5},{8,9},{9,10},{10,1... | collective-permute-start | bytes 589832 | tf_op jit(solution)/shard_map/ppermute | solution.py:86
  29.6 37.2 %collective-permute-start.1 = (bf16[64,1536]{1,0:T(8,128)(2,1)S(1)}, bf16[64,1536]{1,0:T(8,128)(2,1)}, u32[]{:S(2)}, u32[]{:S(2)}) collective-permute-start(bf16[64,1536]{1,0:T(8,128)(2,1)S(1)} %get-tuple-element.35), channel_id=1, source_target_pairs={{0,0},{1,1},{2,3},{3,5},{4,6},{5,2},{6,7},{7,4},{8,8},{9,9},{10,11... | collective-permute-start | bytes 589832 | tf_op jit(solution)/shard_map/ppermute | solution.py:86
  32.0 33.7 %collective-permute-start = (bf16[64,1536]{1,0:T(8,128)(2,1)S(1)}, bf16[64,1536]{1,0:T(8,128)(2,1)}, u32[]{:S(2)}, u32[]{:S(2)}) collective-permute-start(bf16[64,1536]{1,0:T(8,128)(2,1)S(1)} %get-tuple-element.36), channel_id=1, source_target_pairs={{0,0},{1,2},{2,4},{3,5},{4,7},{5,1},{6,6},{7,3},{8,8},{9,10},{10,1... | collective-permute-start | bytes 589832 | tf_op jit(solution)/shard_map/ppermute | solution.py:86
  92.6 23.2 %all-to-all-start = ((bf16[8,128,192]{1,2,0:T(8,128)(2,1)}), bf16[8,128,192]{1,2,0:T(8,128)(2,1)S(1)}, u32[]{:S(2)}, u32[]{:S(2)}) async-start(bf16[8,128,192]{1,2,0:T(8,128)(2,1)} %copy.77), calls=%async_computation | async-start | bytes 786432 | tf_op jit(solution)/shard_map/all_to_all | solution.py:202
  98.9 62.7 %all-gather.11.cloned.1.call-start = ((), (), s32[]{:S(2)}) async-start(), calls=%async_computation.12 | async-start | bytes 3538944 | tf_op jit(solution)/shard_map/all_gather | solution.py:209
  122.7 77.6 %all-gather.13.cloned.1.call-start = ((), (), s32[]{:S(2)}) async-start(), calls=%async_computation.14 | async-start | bytes 3538944 | tf_op jit(solution)/shard_map/all_gather | solution.py:211
  123.3 153.2 %reduce-scatter.9.cloned.1.call-start = ((), (), s32[]{:S(2)}) async-start(), calls=%async_computation.15 | async-start | bytes 3538944 | tf_op jit(solution)/shard_map/reduce_scatter | solution.py:258
  239.2 8.9 %all-to-all-start.1 = ((f32[3,8,128]{2,0,1:T(4,128)}), f32[3,8,128]{2,0,1:T(4,128)}, u32[]{:S(2)}, u32[]{:S(2)}) async-start(f32[3,8,128]{2,0,1:T(4,128)} %bitcast.258), calls=%async_computation.3 | async-start | bytes 32768 | tf_op jit(solution)/shard_map/all_to_all | solution.py:259
  287.7 17.3 %all-to-all-start.2 = ((bf16[128,8,192]{0,2,1:T(8,128)(2,1)}), bf16[128,8,192]{0,2,1:T(8,128)(2,1)}, u32[]{:S(2)}, u32[]{:S(2)}) async-start(bf16[128,8,192]{0,2,1:T(8,128)(2,1)} %bitcast.245), calls=%async_computation.4 | async-start | bytes 786432 | tf_op jit(solution)/shard_map/all_to_all | solution.py:276
  295.8 50.9 %all-gather.15.cloned.1.call-start = ((), (), s32[]{:S(2)}) async-start(), calls=%async_computation.17 | async-start | bytes 3538944 | tf_op jit(solution)/shard_map/all_gather | solution.py:212
  305.1 41.6 %all-to-all-start.3 = ((bf16[128,8,192]{0,2,1:T(8,128)(2,1)}), bf16[128,8,192]{0,2,1:T(8,128)(2,1)}, u32[]{:S(2)}, u32[]{:S(2)}) async-start(bf16[128,8,192]{0,2,1:T(8,128)(2,1)} %bitcast.244), calls=%async_computation.6 | async-start | bytes 786432 | tf_op jit(solution)/shard_map/all_to_all | solution.py:279
  312.4 165.7 %all-reduce.4.cloned.1.call-start = ((), (), s32[]{:S(2)}) async-start(), calls=%async_computation.18 | async-start | bytes 393216 | tf_op jit(solution)/shard_map/psum | solution.py:307
  342.2 200.9 %all-reduce.6.cloned.1.call-start = ((), (), s32[]{:S(2)}) async-start(), calls=%async_computation.22 | async-start | bytes 3145728 | tf_op jit(solution)/shard_map/psum | solution.py:312
  350.7 252.4 %reduce-scatter.17.cloned.1.call-start = ((), (), s32[]{:S(2)}) async-start(), calls=%async_computation.21 | async-start | bytes 5898240 | tf_op jit(solution)/shard_map/reduce_scatter | solution.py:237
  372.4 290.5 %reduce-scatter.15.cloned.1.call-start = ((), (), s32[]{:S(2)}) async-start(), calls=%async_computation.20 | async-start | bytes 5898240 | tf_op jit(solution)/shard_map/reduce_scatter | solution.py:237
  392.4 330.6 %reduce-scatter.13.cloned.1.call-start = ((), (), s32[]{:S(2)}) async-start(), calls=%async_computation.19 | async-start | bytes 5898240 | tf_op jit(solution)/shard_map/reduce_scatter | solution.py:237
  412.4 350.1 %reduce-scatter.11.cloned.1.call-start = ((), (), s32[]{:S(2)}) async-start(), calls=%async_computation.16 | async-start | bytes 3538944 | tf_op jit(solution)/shard_map/reduce_scatter | solution.py:301
  413.0 391.5 %reduce-scatter.7.cloned.1.call-start = ((), (), s32[]{:S(2)}) async-start(), calls=%async_computation.13 | async-start | bytes 3538944 | tf_op jit(solution)/shard_map/reduce_scatter | solution.py:318
  544.5 13.0 %collective-permute-start.5 = (bf16[64,1536]{1,0:T(8,128)(2,1)S(1)}, bf16[64,1536]{1,0:T(8,128)(2,1)S(1)}, u32[]{:S(2)}, u32[]{:S(2)}) collective-permute-start(bf16[64,1536]{1,0:T(8,128)(2,1)S(1)} %get-tuple-element.32), channel_id=1, source_target_pairs={{0,0},{2,1},{4,2},{5,3},{7,4},{1,5},{6,6},{3,7},{8,8},{10,9},{12,1... | collective-permute-start | bytes 589832 | tf_op jit(solution)/shard_map/ppermute | solution.py:86
  547.6 16.9 %collective-permute-start.9 = (bf16[64,1536]{1,0:T(8,128)(2,1)S(1)}, bf16[64,1536]{1,0:T(8,128)(2,1)S(1)}, u32[]{:S(2)}, u32[]{:S(2)}) collective-permute-start(bf16[64,1536]{1,0:T(8,128)(2,1)S(1)} %get-tuple-element.28), channel_id=1, source_target_pairs={{1,0},{3,1},{4,2},{6,3},{0,4},{5,5},{2,6},{7,7},{9,8},{11,9},{12,1... | collective-permute-start | bytes 589832 | tf_op jit(solution)/shard_map/ppermute | solution.py:86
  549.5 15.0 %collective-permute-start.8 = (bf16[64,1536]{1,0:T(8,128)(2,1)S(1)}, bf16[64,1536]{1,0:T(8,128)(2,1)S(1)}, u32[]{:S(2)}, u32[]{:S(2)}) collective-permute-start(bf16[64,1536]{1,0:T(8,128)(2,1)S(1)} %get-tuple-element.29), channel_id=1, source_target_pairs={{0,0},{2,1},{3,2},{5,3},{7,4},{4,5},{1,6},{6,7},{8,8},{10,9},{11,1... | collective-permute-start | bytes 589832 | tf_op jit(solution)/shard_map/ppermute | solution.py:86
  551.4 13.0 %collective-permute-start.7 = (bf16[64,1536]{1,0:T(8,128)(2,1)S(1)}, bf16[64,1536]{1,0:T(8,128)(2,1)S(1)}, u32[]{:S(2)}, u32[]{:S(2)}) collective-permute-start(bf16[64,1536]{1,0:T(8,128)(2,1)S(1)} %get-tuple-element.30), channel_id=1, source_target_pairs={{1,0},{2,1},{4,2},{6,3},{7,4},{3,5},{0,6},{5,7},{9,8},{10,9},{12,1... | collective-permute-start | bytes 589832 | tf_op jit(solution)/shard_map/ppermute | solution.py:86
  553.4 11.0 %collective-permute-start.6 = (bf16[64,1536]{1,0:T(8,128)(2,1)S(1)}, bf16[64,1536]{1,0:T(8,128)(2,1)S(1)}, u32[]{:S(2)}, u32[]{:S(2)}) collective-permute-start(bf16[64,1536]{1,0:T(8,128)(2,1)S(1)} %get-tuple-element.31), channel_id=1, source_target_pairs={{0,0},{1,1},{3,2},{5,3},{6,4},{2,5},{7,6},{4,7},{8,8},{9,9},{11,10... | collective-permute-start | bytes 589832 | tf_op jit(solution)/shard_map/ppermute | solution.py:86
  663.0 141.5 %copy-start.1 = (f32[128,1536]{1,0:T(8,128)S(1)}, f32[128,1536]{1,0:T(8,128)}, u32[]{:S(2)}) copy-start(f32[128,1536]{1,0:T(8,128)} %copy-done) | copy-start | bytes 2359300
  663.0 141.5 %copy-start.5 = (f32[128,1536]{1,0:T(8,128)S(1)}, f32[128,1536]{1,0:T(8,128)}, u32[]{:S(2)}) copy-start(f32[128,1536]{1,0:T(8,128)} %copy-done.4) | copy-start | bytes 2359300
  663.0 141.5 %copy-start.9 = (bf16[128,1536]{1,0:T(8,128)(2,1)S(1)}, bf16[128,1536]{1,0:T(8,128)(2,1)}, u32[]{:S(2)}) copy-start(bf16[128,1536]{1,0:T(8,128)(2,1)} %param.35) | copy-start | bytes 1179652
  663.0 141.5 %copy-start.38 = (f32[128]{0:T(128)S(1)}, f32[128]{0:T(128)}, u32[]{:S(2)}) copy-start(f32[128]{0:T(128)} %copy-done.37) | copy-start | bytes 1540
  663.0 141.5 %copy-start.44 = (f32[128]{0:T(128)S(1)}, f32[128]{0:T(128)}, u32[]{:S(2)}) copy-start(f32[128]{0:T(128)} %copy-done.43) | copy-start | bytes 1540
  (59 other events, 571.3 us)
Sparse Core Ops, SparseCore 0:
  9.6 49.0 all-gather.6
  60.4 56.3 all-gather.8
  122.8 38.7 all-gather.10
  163.1 37.1 all-gather.12
  239.3 37.0 reduce-scatter.8
  297.9 48.2 all-gather.14
  352.3 125.8 all-reduce.3
  482.4 60.7 all-reduce.5
  546.2 56.9 reduce-scatter.16
  606.0 56.9 reduce-scatter.14
  666.0 56.9 reduce-scatter.12
  725.1 37.3 reduce-scatter.10
  764.8 39.6 reduce-scatter.6

commit v2 on v1

--- a/solution.py
+++ b/solution.py
@@ -87,6 +87,38 @@
         for slot, pair in zip(pick, pairs)
     ]
     return jnp.stack(got)[order]
+
+
+def grp_direct(copies):
+    return copies in (2, 4)
+
+
+def grp_send(value, step, copies):
+    return lax.ppermute(value, "grp", [(a, a ^ step) for a in range(copies)])
+
+
+def grp_gather(block, copies, at):
+    if not grp_direct(copies):
+        return lax.all_gather(block, "grp", axis=0, tiled=False)
+    got = jnp.stack([block] + [grp_send(block, d, copies) for d in range(1, copies)])
+    return got[jnp.arange(copies, dtype=jnp.int32) ^ at]
+
+
+def grp_total(value, copies):
+    if not grp_direct(copies):
+        return lax.psum(value, "grp")
+    return value + sum(grp_send(value, d, copies) for d in range(1, copies))
+
+
+def grp_all_sum(rows, copies, at):
+    if not grp_direct(copies):
+        return lax.psum(rows, "grp").astype(f32)
+    blocks = rows.reshape(copies, rows.shape[0] // copies, rows.shape[1])
+    total = lax.dynamic_index_in_dim(blocks, at, 0, keepdims=False).astype(f32)
+    for d in range(1, copies):
+        part = lax.dynamic_index_in_dim(blocks, at ^ d, 0, keepdims=False)
+        total = total + grp_send(part, d, copies).astype(f32)
+    return grp_gather(total.astype(bf16), copies, at).reshape(rows.shape).astype(f32)
 
 
 def local(
@@ -107,6 +139,7 @@
     devices = lax.axis_size("ep")
     me = lax.axis_index("ep")
     copies = lax.axis_size("grp")
+    at = lax.axis_index("grp")
     mine = w_gate.shape[0]
     hidden = w_gate.shape[1]
     experts = mine * devices
@@ -154,10 +187,22 @@
         jnp.int32,
     )[me]
     block_rows = qkv_weight.shape[0] // slots
+    late_qkv, _ = lax.optimization_barrier((qkv_weight, small_all))
     qkv_heads = move_blocks(
-        qkv_weight.reshape(slots, block_rows, width), pick_row, to_heads, order_head
+        late_qkv.reshape(slots, block_rows, width), pick_row, to_heads, order_head
     ).reshape(slots * block_rows, width)
-    full_out = lax.all_gather(out_weight, "ep", axis=0, tiled=True)
+    if grp_direct(copies):
+        out_rows = out_weight.reshape(copies, -1, width)
+        out_quarter = lax.all_gather(
+            lax.dynamic_index_in_dim(out_rows, at, 0, keepdims=False), "ep", axis=0, tiled=False
+        )
+        full_out = grp_gather(out_quarter, copies, at)
+        full_out = full_out.transpose(1, 0, 2, 3).reshape(-1, width)
+    else:
+        full_out = lax.all_gather(out_weight, "ep", axis=0, tiled=True)
+
+    late_cotangent, _ = lax.optimization_barrier((out_cotangent, x_all))
+    g_all = lax.all_gather(late_cotangent, "ep", axis=0, tiled=True)
 
     expert_row = jnp.arange(experts, dtype=jnp.int32)[:, None, None]
     chosen = jnp.any(routes_all[None] == expert_row, axis=1)
@@ -172,6 +217,10 @@
     places = jnp.arange(capacity, dtype=jnp.int32)[None, :, None]
     pick = rank[:, None, :] == places
     pick_low = pick.astype(bf16).reshape(mine * capacity, seq)
+    pick_back = (rank.T[:, :, None] == jnp.arange(capacity, dtype=jnp.int32)[None, None, :]).astype(
+        bf16
+    )
+    pick_back = pick_back.reshape(seq, mine * capacity)
 
     residual_all = x_all.astype(f32)
     scale_one_all = lax.rsqrt(jnp.mean(residual_all * residual_all, axis=-1, keepdims=True) + eps)
@@ -207,8 +256,7 @@
     normed_two = hidden_one * scale_two
     x_two = (normed_two * gain_two).astype(bf16)
     x_two_all = lax.all_gather(x_two, "ep", axis=0, tiled=True)
-    late_cotangent, late_mixed, _ = lax.optimization_barrier((out_cotangent, mixed, x_two))
-    g_all = lax.all_gather(late_cotangent, "ep", axis=0, tiled=True)
+    late_mixed, _ = lax.optimization_barrier((mixed, x_two))
     mixed_all = lax.all_gather(late_mixed, "ep", axis=0, tiled=True)
 
     logits = jnp.einsum("ed,td->et", full_router, x_two_all, preferred_element_type=f32)
@@ -224,21 +272,36 @@
 
     def scatter(rows):
         back = jnp.einsum(
-            "pt,pd->td", pick_low, rows.reshape(mine * capacity, width), preferred_element_type=f32
+            "tp,pd->td", pick_back, rows.reshape(mine * capacity, width), preferred_element_type=f32
         )
         return back.astype(bf16)
 
-    def shares(left, right):
-        grad = jnp.einsum("jcf,jcd->jfd", left, right, preferred_element_type=f32).astype(bf16)
-        grad = grad.reshape(mine * hidden, copies, width // copies).transpose(1, 0, 2)
-        return grad.reshape(copies * mine * hidden, width // copies)
-
-    def grp_sum(part):
-        total = lax.psum_scatter(part, "grp", scatter_dimension=0, tiled=True)
-        return total.astype(f32).reshape(mine, hidden, width // copies)
-
+    cols = width // copies
+
+    def column_blocks(rows):
+        if not grp_direct(copies):
+            return rows
+        return [
+            lax.dynamic_slice_in_dim(rows, (at ^ d) * cols, cols, 2) for d in range(copies)
+        ]
+
+    def shares(left, blocks):
+        if not grp_direct(copies):
+            return jnp.einsum("jcf,jcd->jfd", left, blocks, preferred_element_type=f32).astype(bf16)
+        parts = [
+            jnp.einsum("jcf,jcd->jfd", left, block, preferred_element_type=f32) for block in blocks
+        ]
+        return [parts[0]] + [part.astype(bf16) for part in parts[1:]]
+
+    def grp_sum(parts):
+        if not grp_direct(copies):
+            return lax.psum_scatter(parts, "grp", scatter_dimension=2, tiled=True).astype(f32)
+        got = [grp_send(parts[d], d, copies).astype(f32) for d in range(1, copies)]
+        return parts[0] + sum(got)
+
+    dense_g = gather(g_all)
+    x_two_all, dense_g, pick_back = lax.optimization_barrier((x_two_all, dense_g, pick_back))
     dense_in = gather(x_two_all)
-    dense_g = gather(g_all)
     gate_pre = jnp.einsum("jcd,jfd->jcf", dense_in, w_gate, preferred_element_type=f32)
     up_pre = jnp.einsum("jcd,jfd->jcf", dense_in, w_up, preferred_element_type=f32)
     logistic = jax.nn.sigmoid(gate_pre)
@@ -257,9 +320,14 @@
     back_part = scatter(slot_grad.astype(bf16))
     two_grad = lax.psum_scatter(back_part, "ep", scatter_dimension=0, tiled=True).astype(f32)
     dgate = lax.all_to_all(dgate_own, "ep", split_axis=1, concat_axis=0, tiled=True)
-    down_part = shares(inner, dense_grad)
-    gate_part = shares(gate_back, dense_in)
-    up_part = shares(up_back, dense_in)
+    in_blocks = column_blocks(dense_in)
+    down_part = shares(inner, column_blocks(dense_grad))
+    gate_part = shares(gate_back, in_blocks)
+    up_part = shares(up_back, in_blocks)
+    two_grad, out_part, down_part, gate_part, up_part = lax.optimization_barrier(
+        (two_grad, out_part, down_part, gate_part, up_part)
+    )
+    returned = lax.psum_scatter(out_part, "ep", scatter_dimension=0, tiled=True)
 
     delta = out_cotangent.astype(f32)
     gates_here = lax.dynamic_slice_in_dim(gates, me * tokens, tokens, 1)
@@ -301,21 +369,22 @@
     one_grad = lax.psum_scatter(
         one_part.astype(bf16), "ep", scatter_dimension=0, tiled=True
     ).astype(f32)
-    qkv_grad = jnp.einsum("tc,td->cd", proj_grad, x_low, preferred_element_type=f32)
+    proj_rows = move_blocks(
+        proj_grad.T.reshape(slots, block_rows, seq), pick_head, to_rows, order_row
+    ).reshape(slots * block_rows, seq)
+    qkv_grad = jnp.einsum("ct,td->cd", proj_rows, x_low, preferred_element_type=f32)
     out_grad = jnp.einsum("td,tc->dc", hidden_cols, mixed_all, preferred_element_type=f32)
 
-    small_sum = lax.psum(
-        jnp.concatenate([router_grad, gain_one_grad, gain_two_grad], axis=0), ("grp", "ep")
-    )
-    router_sum = lax.dynamic_slice_in_dim(small_sum[:experts], me * mine, mine, 0)
-    gain_sums = lax.dynamic_slice_in_dim(small_sum[experts:], me * gain_width, gain_width, 1)
-    qkv_sum = lax.psum(qkv_grad.astype(bf16), "grp")
-    qkv_rows = move_blocks(
-        qkv_sum.reshape(slots, block_rows, width), pick_head, to_rows, order_row
-    ).reshape(slots * block_rows, width)
-    out_sum = lax.psum(out_grad.astype(bf16), "grp")
-
-    returned = lax.psum_scatter(out_part, "ep", scatter_dimension=0, tiled=True)
+    gain_pack = jnp.concatenate([gain_one_grad, gain_two_grad], axis=0)
+    gain_pack = gain_pack.reshape(2, devices, gain_width).transpose(1, 0, 2)
+    gain_pack = gain_pack.reshape(devices, 1, 2 * gain_width)
+    gain_pack = jnp.pad(gain_pack, ((0, 0), (0, 0), (0, width - 2 * gain_width)))
+    small_pack = jnp.concatenate([router_grad.reshape(devices, mine, width), gain_pack], axis=1)
+    small_pack = lax.all_to_all(small_pack, "ep", split_axis=0, concat_axis=0, tiled=True)
+    small_sum = grp_total(jnp.sum(small_pack, axis=0), copies)
+    qkv_sum = grp_all_sum(qkv_grad.astype(bf16), copies, at)
+    out_sum = grp_all_sum(out_grad.astype(bf16), copies, at)
+
     layer_out = (hidden_one + returned.astype(f32)).astype(bf16)
     residual = layer_in.astype(f32)
     scale_one = lax.rsqrt(jnp.mean(residual * residual, axis=-1, keepdims=True) + eps)
@@ -325,11 +394,11 @@
     return (
         layer_out,
         grad_in,
-        qkv_rows.astype(f32),
-        out_sum.astype(f32),
-        router_sum,
-        gain_sums[0],
-        gain_sums[1],
+        qkv_sum,
+        out_sum,
+        small_sum[:mine],
+        small_sum[mine, :gain_width],
+        small_sum[mine, gain_width : 2 * gain_width],
         grp_sum(gate_part),
         grp_sum(up_part),
         grp_sum(down_part),

time: 829 us -> 588 us (0.71)
  waiting for transfers between devices: 448 us -> 217 us
  starting transfers between devices: 50.1 us -> 91.9 us
  local copies, waits for them, and re-layouts: 83.2 us -> 46.1 us
  other arithmetic: 42.1 us -> 54.7 us
  matrix products: 134 us -> 122 us
  blocking collectives: 24.4 us -> 12.5 us
    ppermute x0 -> x27, waiting for transfers between devices: none -> 151 us  [grp_send(): return lax.ppermute(value, 'grp', [(a, a ^ step) for a in range(copies)])]
    reduce_scatter x3 -> x0, waiting for transfers between devices: 150 us -> none  [grp_sum(): total = lax.psum_scatter(part, 'grp', scatter_dimension=0, tiled=True)]
    psum x2 -> x0, waiting for transfers between devices: 104 us -> none  [the longest x1 62.7 us: local(): qkv_sum = lax.psum(qkv_grad.astype(bf16), 'grp')]
    reshape x6 -> x2, local copies, waits for them, and re-layouts: 42.6 us -> 0.16 us  [the longest x1 0.1 us: local(): gain_pack = gain_pack.reshape(devices, 1, 2 * gain_width)]
    reduce_scatter x1, waiting for transfers between devices: 40.7 us -> 0.02 us  [local(): returned = lax.psum_scatter(out_part, 'ep', scatter_dimension=0, tiled=True)]
    reduce_scatter x1, waiting for transfers between devices: 36.7 us -> 0.01 us  [local(): lax.psum_scatter(one_part.astype(bf16), 'ep', scatter_dimension=0, tiled=...]
    ppermute x0 -> x27, starting transfers between devices: none -> 32.8 us  [grp_send(): return lax.ppermute(value, 'grp', [(a, a ^ step) for a in range(copies)])]
    reduce_scatter x1, waiting for transfers between devices: 25 us -> 0.02 us  [local(): lax.psum_scatter(back_part, 'ep', scatter_dimension=0, tiled=True)]
  transfers between devices with their start and end apart: 27 -> 50, of which waited for: 15 -> 21; matrix products, arithmetic and copies ran while one was open for 24% -> 30% of each run, Pallas kernels for 0% -> 0%
where the time goes in v2:
time: 588 us; the launch traced here: 577 us
  waiting for transfers between devices  217 us (37%)
  matrix products  122 us (21%)
  starting transfers between devices  91.9 us (16%)
  other arithmetic  54.7 us (9%)
  local copies, waits for them, and re-layouts  46.1 us (8%)
  between operations  33.5 us (6%)
  blocking collectives  12.5 us (2%)
    ppermute x27, waiting for transfers between devices, grp_send(): return lax.ppermute(value, 'grp', [(a, a ^ step) for a in range(copies)])  151 us
    ppermute x27, starting transfers between devices, grp_send(): return lax.ppermute(value, 'grp', [(a, a ^ step) for a in range(copies)])  32.8 us
    dot_general x12, matrix products, shares(): jnp.einsum('jcf,jcd->jfd', left, block, preferred_element_type=f32)  29 us
    ppermute x10, waiting for transfers between devices, move_blocks(): lax.ppermute(lax.dynamic_index_in_dim(blocks, slot, 0, keepdims=False), '...  28.7 us
    all_gather x1, waiting for transfers between devices, local(): x_two_all = lax.all_gather(x_two, 'ep', axis=0, tiled=True)  25.7 us
    ppermute x10, starting transfers between devices, move_blocks(): lax.ppermute(lax.dynamic_index_in_dim(blocks, slot, 0, keepdims=False), '...  23.1 us
    dot_general x2, matrix products, gather(): picked = jnp.einsum('pt,td->pd', pick_low, rows, preferred_element_type=f32)  13.3 us
    all_gather x1, blocking collectives, local(): small_all = lax.all_gather(small, 'ep', axis=0, tiled=False)  12.5 us
  transfers between devices with their start and end apart: 50, of which 21 were waited for; matrix products, arithmetic and copies ran while one was open for 30% of the time, Pallas kernels for 0%

profile of v2, /device:TPU:16, one launch (start us, length us, event | category | flops | bytes accessed | tf_op | source)
XLA Modules:
  0.0 577.1 jit_solution(2828591922810140587)
XLA Ops:
  23.4 12.5 %all-gather = bf16[49152]{0:T(1024)(128)(2,1)S(1)} all-gather(bf16[6144]{0:T(1024)(128)(2,1)S(1)} %concatenate.29), channel_id=2, replica_groups=mesh['grp'=4,'ep'=8] {'ep'}, dimensions={0}, use_global_device_ids=true | all-gather | bytes 110592 | tf_op jit(solution)/shard_map/all_gather | solution.py:165
  39.8 4.9 collective-permute-start
  58.5 4.5 collective-permute-done.1
  63.0 8.1 %collective-permute-done.2 = bf16[64,1536]{1,0:T(8,128)(2,1)S(1)} collective-permute-done((bf16[64,1536]{1,0:T(8,128)(2,1)S(1)}, bf16[64,1536]{1,0:T(8,128)(2,1)S(1)}, u32[]{:S(2)}, u32[]{:S(2)}) %collective-permute-start.2) | collective-permute-done | bytes 196640 | tf_op jit(solution)/shard_map/ppermute | solution.py:86
  74.4 8.3 %collective-permute-done.4 = bf16[64,1536]{1,0:T(8,128)(2,1)S(1)} collective-permute-done((bf16[64,1536]{1,0:T(8,128)(2,1)S(1)}, bf16[64,1536]{1,0:T(8,128)(2,1)S(1)}, u32[]{:S(2)}, u32[]{:S(2)}) %collective-permute-start.4) | collective-permute-done | bytes 196640 | tf_op jit(solution)/shard_map/ppermute | solution.py:86
  94.4 9.6 %fusion.112 = (f32[3,1024]{1,0:T(4,128)S(1)}, f32[3,1024,1024]{1,2,0:T(8,128)}) fusion(pred[1024,1024]{0,1:T(8,128)(4,1)} %fusion.13, bf16[1024,64,1]{0,1,2:T(8,128)(2,1)S(1)} %fusion.77, bf16[1024,4,32]{0,2,1:T(8,128)(2,1)S(1)} %get-tuple-element.60, bf16[1024,4,32]{0,2,1:T(8,128)(2,1)S(1)} %get-tuple-element.61), kind=kOutput, calls=%fused_computation.234 | convolution fusion | flops 419169280 | bytes 15347712 | tf_op jit(solution)/shard_map/sub | solution.py:246
  104.0 6.0 %fusion.22 = bf16[3,1024,64]{1,2,0:T(8,128)(2,1)S(1)} fusion(f32[1024,320]{0,1:T(8,128)} %copy-done.34, f32[3,1024,1024]{1,2,0:T(8,128)} %get-tuple-element.89, f32[3,1024]{1,0:T(4,128)S(1)} %get-tuple-element.88), kind=kOutput, calls=%fused_computation.71 | convolution fusion | flops 409141248 | bytes 13119488 | tf_op jit(solution)/shard_map/hgqk,hkd->hgqd/dot_general | solution.py:249
  110.9 9.3 %all-to-all-start = ((bf16[8,128,192]{1,2,0:T(8,128)(2,1)}), bf16[8,128,192]{1,2,0:T(8,128)(2,1)S(1)}, u32[]{:S(2)}, u32[]{:S(2)}) async-start(bf16[8,128,192]{1,2,0:T(8,128)(2,1)} %copy.118), calls=%async_computation | async-start | bytes 786432 | tf_op jit(solution)/shard_map/all_to_all | solution.py:251
  120.3 19.3 %collective-permute-done.6 = bf16[8,48,1536]{2,1,0:T(8,128)(2,1)} collective-permute-done((bf16[8,48,1536]{2,1,0:T(8,128)(2,1)}, bf16[8,48,1536]{2,1,0:T(8,128)(2,1)}, u32[]{:S(2)}, u32[]{:S(2)}) %collective-permute-start.6) | collective-permute-done | bytes 1179680 | tf_op jit(solution)/shard_map/ppermute | solution.py:97
  139.6 3.6 pad_maximum_fusion
  143.3 5.4 gather_fusion.1
  148.7 4.9 copy.119
  153.6 4.2 multiply_reduce_fusion.3
  163.3 7.3 %convolution_convert_fusion.1 = bf16[1152,1536]{1,0:T(8,128)(2,1)} fusion(pred[1152,1024]{1,0:T(32,128)(4,1)S(1)} %bitcast_compare_fusion.1, bf16[1024,1536]{1,0:T(8,128)(2,1)} %all-gather.13.cloned.1.call-done), kind=kOutput, calls=%fused_computation.16 | convolution fusion | flops 3625648128 | bytes 7864320 | tf_op jit(solution)/shard_map/pt,td->pd/dot_general | solution.py:270
  170.5 25.7 %all-gather.11.cloned.1.call-done = bf16[1024,1536]{1,0:T(8,128)(2,1)} async-done(((bf16[128,1536]{1,0:T(8,128)(2,1)}), bf16[1024,1536]{1,0:T(8,128)(2,1)}) %all-gather.11.cloned.1.call-update) | async-done | bytes 3145744 | tf_op jit(solution)/shard_map/all_gather | solution.py:258
  196.2 6.0 %convolution_convert_fusion = bf16[1152,1536]{1,0:T(8,128)(2,1)S(1)} fusion(pred[1152,1024]{1,0:T(32,128)(4,1)S(1)} %bitcast_compare_fusion.1, bf16[1024,1536]{1,0:T(8,128)(2,1)} %all-gather.11.cloned.1.call-done), kind=kOutput, calls=%fused_computation.15 | convolution fusion | flops 3625648128 | bytes 7864320 | tf_op jit(solution)/shard_map/pt,td->pd/dot_general | solution.py:270
  217.2 6.2 %multiply_convert_fusion.3 = (bf16[3,384,512]{2,1,0:T(8,128)(2,1)S(1)}, bf16[3,384,512]{2,1,0:T(8,128)(2,1)S(1)}) fusion(f32[3,384,512]{2,1,0:T(8,128)S(1)} %copy-done.62, f32[3,384,512]{2,1,0:T(8,128)} %get-tuple-element.93, bf16[3,384,1536]{2,1,0:T(8,128)(2,1)S(1)} %get-tuple-element.84, bf16[3,512,1536]{2,1,0:T(8,128)(2,1)S(1)} %bitcast.290), kind=kOutput, calls=%fused_computation.56 | convolution fusion | flops 1819607040 | bytes 15335424 | tf_op jit(solution)/shard_map/jcd,jfd->jcf/dot_general | solution.py:314
  227.5 5.8 %convolution_convert_fusion.3 = bf16[1024,1536]{1,0:T(8,128)(2,1)} fusion(bf16[1024,1152]{0,1:T(8,128)(2,1)S(1)} %copy-done.26, bf16[1152,1536]{1,0:T(8,128)(2,1)S(1)} %bitcast.303), kind=kOutput, calls=%fused_computation.42 | convolution fusion | flops 3625451520 | bytes 9043968 | tf_op jit(solution)/shard_map/tp,pd->td/dot_general | solution.py:274
  233.4 5.1 all-to-all-start.1
  264.4 6.1 %convolution_convert_fusion.2 = bf16[1024,1536]{1,0:T(8,128)(2,1)} fusion(bf16[1024,1152]{0,1:T(8,128)(2,1)S(1)} %copy-done.27, bf16[1152,1536]{1,0:T(8,128)(2,1)S(1)} %bitcast.300), kind=kOutput, calls=%fused_computation.41 | convolution fusion | flops 3625451520 | bytes 9043968 | tf_op jit(solution)/shard_map/tp,pd->td/dot_general | solution.py:274
  279.8 5.1 all-to-all-start.2
  285.5 8.6 %all-to-all-done.2 = bf16[128,8,192]{0,2,1:T(8,128)(2,1)S(1)} async-done(((bf16[128,8,192]{0,2,1:T(8,128)(2,1)}), bf16[128,8,192]{0,2,1:T(8,128)(2,1)S(1)}, u32[]{:S(2)}, u32[]{:S(2)}) %all-to-all-start.2) | async-done | bytes 393248 | tf_op jit(solution)/shard_map/all_to_all | solution.py:344
  294.6 6.3 %multiply_reduce_fusion = (f32[3,1024]{1,0:T(4,128)S(1)}, f32[3,1024,1024]{1,2,0:T(8,128)S(1)}) fusion(f32[3,1024,1024]{1,2,0:T(8,128)} %get-tuple-element.89, f32[3,1024]{1,0:T(4,128)S(1)} %copy-done.46, f32[1024,320]{0,1:T(8,128)} %copy-done.34, bf16[1024,1,3,64]{0,3,2,1:T(8,128)(2,1)S(1)} %reshape.428), kind=kOutput, calls=%fused_computation.7 | convolution fusion | flops 412087296 | bytes 25714688 | tf_op jit(solution)/shard_map/hgqd,hkd->hgqk/dot_general | solution.py:350
  300.9 8.2 %multiply_convert_fusion = bf16[3,1024,1024]{1,2,0:T(8,128)(2,1)S(1)} fusion(f32[3,1024,1024]{1,2,0:T(8,128)S(1)} %get-tuple-element.100, f32[3,1024]{1,0:T(4,128)S(1)} %get-tuple-element.99, f32[3,1024,1024]{1,2,0:T(8,128)} %get-tuple-element.89, f32[3,1024]{1,0:T(4,128)S(1)} %copy-done.46), kind=kLoop, calls=%fused_computation.6 | loop fusion | flops 12582912 | bytes 31481856 | tf_op jit(solution)/shard_map/convert_element_type | solution.py:352
  315.0 3.8 fusion.7
  335.1 7.0 %all-to-all-start.3 = ((bf16[128,8,192]{0,2,1:T(8,128)(2,1)}), bf16[128,8,192]{0,2,1:T(8,128)(2,1)}, u32[]{:S(2)}, u32[]{:S(2)}) async-start(bf16[128,8,192]{0,2,1:T(8,128)(2,1)} %bitcast.95), calls=%async_computation.6 | async-start | bytes 786432 | tf_op jit(solution)/shard_map/all_to_all | solution.py:347
  357.3 9.0 %all-to-all-start.4 = ((f32[8,4,1536]{2,1,0:T(4,128)}), f32[8,4,1536]{2,1,0:T(4,128)S(1)}, u32[]{:S(2)}, u32[]{:S(2)}) async-start(f32[8,4,1536]{2,1,0:T(4,128)} %select_maximum_fusion), calls=%async_computation.7 | async-start | bytes 393216 | tf_op jit(solution)/shard_map/all_to_all | solution.py:383
  399.7 7.6 %collective-permute-done.23 = bf16[48,1536]{1,0:T(8,128)(2,1)S(1)} collective-permute-done((bf16[48,1536]{1,0:T(8,128)(2,1)S(1)}, bf16[48,1536]{1,0:T(8,128)(2,1)S(1)}, u32[]{:S(2)}, u32[]{:S(2)}) %collective-permute-start.23) | collective-permute-done | bytes 147488 | tf_op jit(solution)/shard_map/ppermute | solution.py:97
  420.2 51.9 %collective-permute-done.13 = bf16[80,1536]{1,0:T(8,128)(2,1)S(1)} collective-permute-done((bf16[80,1536]{1,0:T(8,128)(2,1)}, bf16[80,1536]{1,0:T(8,128)(2,1)S(1)}, u32[]{:S(2)}, u32[]{:S(2)}) %collective-permute-start.13) | collective-permute-done | bytes 245792 | tf_op jit(solution)/shard_map/ppermute | solution.py:97
  480.5 4.0 add_add_fusion.2
  484.5 40.4 %collective-permute-done.32 = bf16[3,512,384]{2,1,0:T(8,128)(2,1)S(1)} collective-permute-done((bf16[3,512,384]{2,1,0:T(8,128)(2,1)}, bf16[3,512,384]{2,1,0:T(8,128)(2,1)S(1)}, u32[]{:S(2)}, u32[]{:S(2)}) %collective-permute-start.32) | collective-permute-done | bytes 1179680 | tf_op jit(solution)/shard_map/ppermute | solution.py:97
  530.3 22.3 %collective-permute-done.35 = bf16[3,512,384]{2,1,0:T(8,128)(2,1)S(1)} collective-permute-done((bf16[3,512,384]{2,1,0:T(8,128)(2,1)}, bf16[3,512,384]{2,1,0:T(8,128)(2,1)S(1)}, u32[]{:S(2)}, u32[]{:S(2)}) %collective-permute-start.35) | collective-permute-done | bytes 1179680 | tf_op jit(solution)/shard_map/ppermute | solution.py:97
  (385 shorter events, 206.6 us)
Async XLA Ops:
  7.2 77.2 %all-gather.9.cloned.1.call-start = ((), (), s32[]{:S(2)}) async-start(), calls=%async_computation.9 | async-start | bytes 1327104 | tf_op jit(solution)/shard_map/all_gather | solution.py:196
  8.9 78.9 %all-gather.7.cloned.1.call-start = ((), (), s32[]{:S(2)}) async-start(), calls=%async_computation.8 | async-start | bytes 3538944 | tf_op jit(solution)/shard_map/all_gather | solution.py:154
  9.7 153.5 %all-gather.13.cloned.1.call-start = ((), (), s32[]{:S(2)}) async-start(), calls=%async_computation.11 | async-start | bytes 3538944 | tf_op jit(solution)/shard_map/all_gather | solution.py:205
  48.5 26.0 %collective-permute-start.3 = (bf16[64,1536]{1,0:T(8,128)(2,1)S(1)}, bf16[64,1536]{1,0:T(8,128)(2,1)S(1)}, u32[]{:S(2)}, u32[]{:S(2)}) collective-permute-start(bf16[64,1536]{1,0:T(8,128)(2,1)S(1)} %get-tuple-element.65), channel_id=1, source_target_pairs={{0,0},{1,2},{2,3},{3,5},{4,7},{5,4},{6,1},{7,6},{8,8},{9,10},{10,1... | collective-permute-start | bytes 589832 | tf_op jit(solution)/shard_map/ppermute | solution.py:86
  51.3 31.4 %collective-permute-start.4 = (bf16[64,1536]{1,0:T(8,128)(2,1)S(1)}, bf16[64,1536]{1,0:T(8,128)(2,1)S(1)}, u32[]{:S(2)}, u32[]{:S(2)}) collective-permute-start(bf16[64,1536]{1,0:T(8,128)(2,1)S(1)} %slice.66), channel_id=1, source_target_pairs={{0,1},{1,3},{2,4},{3,6},{4,0},{5,5},{6,2},{7,7},{8,9},{9,11},{10,1... | collective-permute-start | bytes 589832 | tf_op jit(solution)/shard_map/ppermute | solution.py:86
  84.4 35.9 %collective-permute-start.7 = (bf16[8,48,1536]{2,1,0:T(8,128)(2,1)}, bf16[8,48,1536]{2,1,0:T(8,128)(2,1)S(1)}, u32[]{:S(2)}, u32[]{:S(2)}) collective-permute-start(bf16[8,48,1536]{2,1,0:T(8,128)(2,1)} %all-gather.9.cloned.1.call-done), channel_id=1, source_target_pairs={{0,24},{8,16},{16,8},{24,0},{1,25},{9,17},{17,9},{25,1},{2,26},{10... | collective-permute-start | bytes 3538952 | tf_op jit(solution)/shard_map/ppermute | solution.py:97
  87.0 52.7 %collective-permute-start.6 = (bf16[8,48,1536]{2,1,0:T(8,128)(2,1)}, bf16[8,48,1536]{2,1,0:T(8,128)(2,1)}, u32[]{:S(2)}, u32[]{:S(2)}) collective-permute-start(bf16[8,48,1536]{2,1,0:T(8,128)(2,1)} %all-gather.9.cloned.1.call-done), channel_id=1, source_target_pairs={{0,16},{8,24},{16,0},{24,8},{1,17},{9,25},{17,1},{25,9},{2,18},{10... | collective-permute-start | bytes 3538952 | tf_op jit(solution)/shard_map/ppermute | solution.py:97
  87.5 52.1 %collective-permute-start.5 = (bf16[8,48,1536]{2,1,0:T(8,128)(2,1)}, bf16[8,48,1536]{2,1,0:T(8,128)(2,1)}, u32[]{:S(2)}, u32[]{:S(2)}) collective-permute-start(bf16[8,48,1536]{2,1,0:T(8,128)(2,1)} %all-gather.9.cloned.1.call-done), channel_id=1, source_target_pairs={{0,8},{8,0},{16,24},{24,16},{1,9},{9,1},{17,25},{25,17},{2,10},{10... | collective-permute-start | bytes 3538952 | tf_op jit(solution)/shard_map/ppermute | solution.py:97
  110.9 42.7 %all-to-all-start = ((bf16[8,128,192]{1,2,0:T(8,128)(2,1)}), bf16[8,128,192]{1,2,0:T(8,128)(2,1)S(1)}, u32[]{:S(2)}, u32[]{:S(2)}) async-start(bf16[8,128,192]{1,2,0:T(8,128)(2,1)} %copy.118), calls=%async_computation | async-start | bytes 786432 | tf_op jit(solution)/shard_map/all_to_all | solution.py:251
  120.2 76.0 %all-gather.11.cloned.1.call-start = ((), (), s32[]{:S(2)}) async-start(), calls=%async_computation.10 | async-start | bytes 3538944 | tf_op jit(solution)/shard_map/all_gather | solution.py:258
  159.7 114.2 %reduce-scatter.4.cloned.1.call-start = ((), (), s32[]{:S(2)}) async-start(), calls=%async_computation.12 | async-start | bytes 3538944 | tf_op jit(solution)/shard_map/reduce_scatter | solution.py:321
  233.4 40.4 %all-to-all-start.1 = ((f32[3,8,128]{2,0,1:T(4,128)}), f32[3,8,128]{2,0,1:T(4,128)S(1)}, u32[]{:S(2)}, u32[]{:S(2)}) async-start(f32[3,8,128]{2,0,1:T(4,128)} %bitcast.48), calls=%async_computation.3 | async-start | bytes 32768 | tf_op jit(solution)/shard_map/all_to_all | solution.py:322
  284.9 81.4 %all-gather.15.cloned.1.call-start = ((), (), s32[]{:S(2)}) async-start(), calls=%async_computation.15 | async-start | bytes 3538944 | tf_op jit(solution)/shard_map/all_gather | solution.py:260
  285.5 280.7 %reduce-scatter.8.cloned.1.call-start = ((), (), s32[]{:S(2)}) async-start(), calls=%async_computation.14 | async-start | bytes 3538944 | tf_op jit(solution)/shard_map/reduce_scatter | solution.py:369
  342.1 225.3 %reduce-scatter.6.cloned.1.call-start = ((), (), s32[]{:S(2)}) async-start(), calls=%async_computation.13 | async-start | bytes 3538944 | tf_op jit(solution)/shard_map/reduce_scatter | solution.py:330
  342.5 131.6 %collective-permute-start.30 = (bf16[3,512,384]{2,1,0:T(8,128)(2,1)}, bf16[3,512,384]{2,1,0:T(8,128)(2,1)}, u32[]{:S(2)}, u32[]{:S(2)}) collective-permute-start(bf16[3,512,384]{2,1,0:T(8,128)(2,1)} %convolution_convert_fusion.10), channel_id=1, source_target_pairs={{0,24},{8,16},{16,8},{24,0},{1,25},{9,17},{17,9},{25,1},{2,26},{10... | collective-permute-start | bytes 3538952 | tf_op jit(solution)/shard_map/ppermute | solution.py:97
  349.2 25.4 %collective-permute-start.9 = (bf16[64,1024]{1,0:T(8,128)(2,1)}, bf16[64,1024]{1,0:T(8,128)(2,1)}, u32[]{:S(2)}, u32[]{:S(2)}) collective-permute-start(bf16[64,1024]{1,0:T(8,128)(2,1)} %get-tuple-element.74), channel_id=1, source_target_pairs={{0,0},{1,1},{3,2},{5,3},{6,4},{2,5},{7,6},{4,7},{8,8},{9,9},{11,10... | collective-permute-start | bytes 393224 | tf_op jit(solution)/shard_map/ppermute | solution.py:86
  352.3 26.2 %collective-permute-start.10 = (bf16[64,1024]{1,0:T(8,128)(2,1)}, bf16[64,1024]{1,0:T(8,128)(2,1)}, u32[]{:S(2)}, u32[]{:S(2)}) collective-permute-start(bf16[64,1024]{1,0:T(8,128)(2,1)} %get-tuple-element.73), channel_id=1, source_target_pairs={{1,0},{2,1},{4,2},{6,3},{7,4},{3,5},{0,6},{5,7},{9,8},{10,9},{12,1... | collective-permute-start | bytes 393224 | tf_op jit(solution)/shard_map/ppermute | solution.py:86
  352.4 27.6 %collective-permute-start.11 = (bf16[64,1024]{1,0:T(8,128)(2,1)}, bf16[64,1024]{1,0:T(8,128)(2,1)}, u32[]{:S(2)}, u32[]{:S(2)}) collective-permute-start(bf16[64,1024]{1,0:T(8,128)(2,1)} %get-tuple-element.72), channel_id=1, source_target_pairs={{0,0},{2,1},{3,2},{5,3},{7,4},{4,5},{1,6},{6,7},{8,8},{10,9},{11,1... | collective-permute-start | bytes 393224 | tf_op jit(solution)/shard_map/ppermute | solution.py:86
  357.3 39.7 %all-to-all-start.4 = ((f32[8,4,1536]{2,1,0:T(4,128)}), f32[8,4,1536]{2,1,0:T(4,128)S(1)}, u32[]{:S(2)}, u32[]{:S(2)}) async-start(f32[8,4,1536]{2,1,0:T(4,128)} %select_maximum_fusion), calls=%async_computation.7 | async-start | bytes 393216 | tf_op jit(solution)/shard_map/all_to_all | solution.py:383
  414.2 61.6 %collective-permute-start.29 = (bf16[3,512,384]{2,1,0:T(8,128)(2,1)}, bf16[3,512,384]{2,1,0:T(8,128)(2,1)S(1)}, u32[]{:S(2)}, u32[]{:S(2)}) collective-permute-start(bf16[3,512,384]{2,1,0:T(8,128)(2,1)} %convolution_convert_fusion.11), channel_id=1, source_target_pairs={{0,16},{8,24},{16,0},{24,8},{1,17},{9,25},{17,1},{25,9},{2,18},{10... | collective-permute-start | bytes 3538952 | tf_op jit(solution)/shard_map/ppermute | solution.py:97
  416.3 60.7 %collective-permute-start.28 = (bf16[3,512,384]{2,1,0:T(8,128)(2,1)}, bf16[3,512,384]{2,1,0:T(8,128)(2,1)S(1)}, u32[]{:S(2)}, u32[]{:S(2)}) collective-permute-start(bf16[3,512,384]{2,1,0:T(8,128)(2,1)} %convolution_convert_fusion.12), channel_id=1, source_target_pairs={{0,8},{8,0},{16,24},{24,16},{1,9},{9,1},{17,25},{25,17},{2,10},{10... | collective-permute-start | bytes 3538952 | tf_op jit(solution)/shard_map/ppermute | solution.py:97
  417.3 61.7 %collective-permute-start.33 = (bf16[3,512,384]{2,1,0:T(8,128)(2,1)}, bf16[3,512,384]{2,1,0:T(8,128)(2,1)S(1)}, u32[]{:S(2)}, u32[]{:S(2)}) collective-permute-start(bf16[3,512,384]{2,1,0:T(8,128)(2,1)} %convolution_convert_fusion.7), channel_id=1, source_target_pairs={{0,24},{8,16},{16,8},{24,0},{1,25},{9,17},{17,9},{25,1},{2,26},{10... | collective-permute-start | bytes 3538952 | tf_op jit(solution)/shard_map/ppermute | solution.py:97
  418.9 53.2 %collective-permute-start.13 = (bf16[80,1536]{1,0:T(8,128)(2,1)}, bf16[80,1536]{1,0:T(8,128)(2,1)S(1)}, u32[]{:S(2)}, u32[]{:S(2)}) collective-permute-start(bf16[80,1536]{1,0:T(8,128)(2,1)} %get-tuple-element.62), channel_id=1, source_target_pairs={{0,8},{8,0},{16,24},{24,16},{1,9},{9,1},{17,25},{25,17},{2,10},{10... | collective-permute-start | bytes 737288 | tf_op jit(solution)/shard_map/ppermute | solution.py:97
  472.1 52.8 %collective-permute-start.32 = (bf16[3,512,384]{2,1,0:T(8,128)(2,1)}, bf16[3,512,384]{2,1,0:T(8,128)(2,1)S(1)}, u32[]{:S(2)}, u32[]{:S(2)}) collective-permute-start(bf16[3,512,384]{2,1,0:T(8,128)(2,1)} %convolution_convert_fusion.8), channel_id=1, source_target_pairs={{0,16},{8,24},{16,0},{24,8},{1,17},{9,25},{17,1},{25,9},{2,18},{10... | collective-permute-start | bytes 3538952 | tf_op jit(solution)/shard_map/ppermute | solution.py:97
  474.1 52.5 %collective-permute-start.31 = (bf16[3,512,384]{2,1,0:T(8,128)(2,1)}, bf16[3,512,384]{2,1,0:T(8,128)(2,1)S(1)}, u32[]{:S(2)}, u32[]{:S(2)}) collective-permute-start(bf16[3,512,384]{2,1,0:T(8,128)(2,1)} %convolution_convert_fusion.9), channel_id=1, source_target_pairs={{0,8},{8,0},{16,24},{24,16},{1,9},{9,1},{17,25},{25,17},{2,10},{10... | collective-permute-start | bytes 3538952 | tf_op jit(solution)/shard_map/ppermute | solution.py:97
  475.7 53.9 %collective-permute-start.36 = (bf16[3,512,384]{2,1,0:T(8,128)(2,1)}, bf16[3,512,384]{2,1,0:T(8,128)(2,1)S(1)}, u32[]{:S(2)}, u32[]{:S(2)}) collective-permute-start(bf16[3,512,384]{2,1,0:T(8,128)(2,1)} %convolution_convert_fusion.13), channel_id=1, source_target_pairs={{0,24},{8,16},{16,8},{24,0},{1,25},{9,17},{17,9},{25,1},{2,26},{10... | collective-permute-start | bytes 3538952 | tf_op jit(solution)/shard_map/ppermute | solution.py:97
  477.0 75.5 %collective-permute-start.35 = (bf16[3,512,384]{2,1,0:T(8,128)(2,1)}, bf16[3,512,384]{2,1,0:T(8,128)(2,1)S(1)}, u32[]{:S(2)}, u32[]{:S(2)}) collective-permute-start(bf16[3,512,384]{2,1,0:T(8,128)(2,1)} %convolution_convert_fusion.14), channel_id=1, source_target_pairs={{0,16},{8,24},{16,0},{24,8},{1,17},{9,25},{17,1},{25,9},{2,18},{10... | collective-permute-start | bytes 3538952 | tf_op jit(solution)/shard_map/ppermute | solution.py:97
  479.0 74.7 %collective-permute-start.34 = (bf16[3,512,384]{2,1,0:T(8,128)(2,1)}, bf16[3,512,384]{2,1,0:T(8,128)(2,1)S(1)}, u32[]{:S(2)}, u32[]{:S(2)}) collective-permute-start(bf16[3,512,384]{2,1,0:T(8,128)(2,1)} %convolution_convert_fusion.15), channel_id=1, source_target_pairs={{0,8},{8,0},{16,24},{24,16},{1,9},{9,1},{17,25},{25,17},{2,10},{10... | collective-permute-start | bytes 3538952 | tf_op jit(solution)/shard_map/ppermute | solution.py:97
  524.9 32.1 %collective-permute-start.18 = (bf16[80,1536]{1,0:T(8,128)(2,1)S(1)}, bf16[80,1536]{1,0:T(8,128)(2,1)S(1)}, u32[]{:S(2)}, u32[]{:S(2)}) collective-permute-start(bf16[80,1536]{1,0:T(8,128)(2,1)S(1)} %fusion.65), channel_id=1, source_target_pairs={{0,24},{8,16},{16,8},{24,0},{1,25},{9,17},{17,9},{25,1},{2,26},{10... | collective-permute-start | bytes 737288 | tf_op jit(solution)/shard_map/ppermute | solution.py:97
  526.6 31.2 %collective-permute-start.17 = (bf16[80,1536]{1,0:T(8,128)(2,1)S(1)}, bf16[80,1536]{1,0:T(8,128)(2,1)S(1)}, u32[]{:S(2)}, u32[]{:S(2)}) collective-permute-start(bf16[80,1536]{1,0:T(8,128)(2,1)S(1)} %fusion.65), channel_id=1, source_target_pairs={{0,16},{8,24},{16,0},{24,8},{1,17},{9,25},{17,1},{25,9},{2,18},{10... | collective-permute-start | bytes 737288 | tf_op jit(solution)/shard_map/ppermute | solution.py:97
  529.6 29.7 %collective-permute-start.16 = (bf16[80,1536]{1,0:T(8,128)(2,1)S(1)}, bf16[80,1536]{1,0:T(8,128)(2,1)S(1)}, u32[]{:S(2)}, u32[]{:S(2)}) collective-permute-start(bf16[80,1536]{1,0:T(8,128)(2,1)S(1)} %fusion.65), channel_id=1, source_target_pairs={{0,8},{8,0},{16,24},{24,16},{1,9},{9,1},{17,25},{25,17},{2,10},{10... | collective-permute-start | bytes 737288 | tf_op jit(solution)/shard_map/ppermute | solution.py:97
  (95 other events, 1154.7 us)
Sparse Core Ops, SparseCore 0:
  10.2 23.5 all-gather.8
  35.5 50.9 all-gather.6
  88.1 48.4 all-gather.12
  159.8 36.3 all-gather.10
  233.5 36.9 reduce-scatter.3
  287.0 39.9 all-gather.14
  329.2 61.9 reduce-scatter.7
  393.5 37.0 reduce-scatter.5

commit v3 on v2

--- a/solution.py
+++ b/solution.py
@@ -3,10 +3,12 @@
 from jax import lax
 from jax.sharding import PartitionSpec as P
 
+
 QUERY_HEADS = 24
 KEY_VALUE_HEADS = 8
 HEAD_DIMENSION = 64
 TOPK = 8
+
 
 eps = 1e-06
 theta = 10000.0
@@ -82,11 +84,8 @@
 
 
 def move_blocks(blocks, pick, pairs, order):
-    got = [
-        lax.ppermute(lax.dynamic_index_in_dim(blocks, slot, 0, keepdims=False), "ep", pair)
-        for slot, pair in zip(pick, pairs)
-    ]
-    return jnp.stack(got)[order]
+    chosen = blocks[pick]
+    return jnp.stack([lax.ppermute(chosen[p], "ep", pair) for p, pair in enumerate(pairs)])[order]
 
 
 def grp_direct(copies):
@@ -176,30 +175,33 @@
     slots = len(rounds)
     to_heads = [[(i, t[i]) for i in range(devices)] for _, t, _ in rounds]
     to_rows = [[(b, a) for a, b in pair] for pair in to_heads]
-    pick_row = [jnp.array(s, jnp.int32)[me] for s, _, _ in rounds]
-    pick_head = [jnp.array(s, jnp.int32)[me] for _, _, s in rounds]
-    order_head = jnp.array(
-        [[[r[2][d] for r in rounds].index(s) for s in range(slots)] for d in range(devices)],
-        jnp.int32,
-    )[me]
-    order_row = jnp.array(
-        [[[r[0][d] for r in rounds].index(s) for s in range(slots)] for d in range(devices)],
-        jnp.int32,
-    )[me]
+    table = []
+    for d in range(devices):
+        put = [[r[2][d] for r in rounds].index(s) for s in range(slots)]
+        back = [[r[0][d] for r in rounds].index(s) for s in range(slots)]
+        table.append([r[0][d] for r in rounds] + [r[2][d] for r in rounds] + put + back)
+    row = jnp.array(table, jnp.int32)[me]
+    pick_row, pick_head, order_head, order_row = (
+        row[n * slots : (n + 1) * slots] for n in range(4)
+    )
     block_rows = qkv_weight.shape[0] // slots
     late_qkv, _ = lax.optimization_barrier((qkv_weight, small_all))
     qkv_heads = move_blocks(
         late_qkv.reshape(slots, block_rows, width), pick_row, to_heads, order_head
     ).reshape(slots * block_rows, width)
     if grp_direct(copies):
-        out_rows = out_weight.reshape(copies, -1, width)
-        out_quarter = lax.all_gather(
-            lax.dynamic_index_in_dim(out_rows, at, 0, keepdims=False), "ep", axis=0, tiled=False
-        )
-        full_out = grp_gather(out_quarter, copies, at)
-        full_out = full_out.transpose(1, 0, 2, 3).reshape(-1, width)
+        out_cols = out_weight.shape[1] // copies
+        out_quarter = lax.dynamic_slice_in_dim(out_weight, at * out_cols, out_cols, 1)
+        out_quarter = lax.all_gather(out_quarter, "ep", axis=0, tiled=True)
+        out_parts = [out_quarter] + [grp_send(out_quarter, d, copies) for d in range(1, copies)]
+        spans = [(at ^ d) * out_cols for d in range(copies)]
+        ordered = jnp.arange(copies, dtype=jnp.int32) ^ at
     else:
-        full_out = lax.all_gather(out_weight, "ep", axis=0, tiled=True)
+        out_cols = out_weight.shape[1]
+        out_parts = [lax.all_gather(out_weight, "ep", axis=0, tiled=True)]
+        spans = [0]
+        ordered = jnp.zeros((1,), jnp.int32)
+    w_pair = jnp.concatenate([w_gate, w_up], axis=1)
 
     late_cotangent, _ = lax.optimization_barrier((out_cotangent, x_all))
     g_all = lax.all_gather(late_cotangent, "ep", axis=0, tiled=True)
@@ -250,8 +252,10 @@
     mixed_heads = attended.transpose(2, 0, 1, 3).reshape(seq, heads * hd).astype(bf16)
     mixed = lax.all_to_all(mixed_heads, "ep", split_axis=0, concat_axis=1, tiled=True)
 
-    branch = jnp.einsum("tc,dc->td", mixed, full_out, preferred_element_type=f32)
-    hidden_one = layer_in.astype(f32) + branch
+    hidden_one = layer_in.astype(f32)
+    for start, part in zip(spans, out_parts):
+        piece = lax.dynamic_slice_in_dim(mixed, start, out_cols, 1)
+        hidden_one = hidden_one + jnp.einsum("tc,dc->td", piece, part, preferred_element_type=f32)
     scale_two = lax.rsqrt(jnp.mean(hidden_one * hidden_one, axis=-1, keepdims=True) + eps)
     normed_two = hidden_one * scale_two
     x_two = (normed_two * gain_two).astype(bf16)
@@ -278,55 +282,61 @@
 
     cols = width // copies
 
-    def column_blocks(rows):
+    def grad_rows(left, right, first):
         if not grp_direct(copies):
-            return rows
-        return [
-            lax.dynamic_slice_in_dim(rows, (at ^ d) * cols, cols, 2) for d in range(copies)
-        ]
-
-    def shares(left, blocks):
+            part = jnp.einsum("jcf,jcd->jfd", left, right, preferred_element_type=f32)
+            part = part.astype(bf16)
+            return lax.psum_scatter(part, "grp", scatter_dimension=2, tiled=True).astype(f32)
+
+        def block(step):
+            return lax.dynamic_slice_in_dim(right, (at ^ step) * cols, cols, 2)
+
+        if copies == 2:
+            away, stay = block(1), block(0)
+        else:
+            second = 3 - first
+            away = jnp.concatenate([block(first), block(3)], axis=2)
+            stay = jnp.concatenate([block(0), block(second)], axis=2)
+        away = jnp.einsum("jcf,jcd->jfd", left, away, preferred_element_type=f32).astype(bf16)
+        got = grp_send(away, first, copies)
+        kept = jnp.einsum("jcf,jcd->jfd", left, stay, preferred_element_type=f32)
+        return kept, got
+
+    def grad_finish(state, first):
         if not grp_direct(copies):
-            return jnp.einsum("jcf,jcd->jfd", left, blocks, preferred_element_type=f32).astype(bf16)
-        parts = [
-            jnp.einsum("jcf,jcd->jfd", left, block, preferred_element_type=f32) for block in blocks
-        ]
-        return [parts[0]] + [part.astype(bf16) for part in parts[1:]]
-
-    def grp_sum(parts):
-        if not grp_direct(copies):
-            return lax.psum_scatter(parts, "grp", scatter_dimension=2, tiled=True).astype(f32)
-        got = [grp_send(parts[d], d, copies).astype(f32) for d in range(1, copies)]
-        return parts[0] + sum(got)
+            return state
+        kept, got = state
+        total = kept + got.astype(f32)
+        if copies == 2:
+            return total
+        passed = grp_send(total[:, :, cols:].astype(bf16), 3 - first, copies)
+        return total[:, :, :cols] + passed.astype(f32)
 
     dense_g = gather(g_all)
     x_two_all, dense_g, pick_back = lax.optimization_barrier((x_two_all, dense_g, pick_back))
     dense_in = gather(x_two_all)
-    gate_pre = jnp.einsum("jcd,jfd->jcf", dense_in, w_gate, preferred_element_type=f32)
-    up_pre = jnp.einsum("jcd,jfd->jcf", dense_in, w_up, preferred_element_type=f32)
+    pair_pre = jnp.einsum("jcd,jfd->jcf", dense_in, w_pair, preferred_element_type=f32)
+    gate_pre, up_pre = pair_pre[:, :, :hidden], pair_pre[:, :, hidden:]
     logistic = jax.nn.sigmoid(gate_pre)
     inner = (gate_pre * logistic * up_pre).astype(bf16)
     expert_out = jnp.einsum("jcf,jfd->jcd", inner, w_down, preferred_element_type=f32)
     place_dgate = jnp.sum(expert_out * dense_g.astype(f32), axis=-1)
     dgate_own = jnp.sum(jnp.where(pick, place_dgate[:, :, None], 0.0), axis=1)
-    out_part = scatter((place_gate * expert_out).astype(bf16))
     dense_grad = (place_gate * dense_g.astype(f32)).astype(bf16)
     inner_grad = jnp.einsum("jcd,jfd->jcf", dense_grad, w_down, preferred_element_type=f32)
     gate_back = (inner_grad * up_pre * logistic * (1.0 + gate_pre * (1.0 - logistic))).astype(bf16)
     up_back = (inner_grad * gate_pre * logistic).astype(bf16)
-    slot_grad = jnp.einsum(
-        "jcf,jfd->jcd", gate_back, w_gate, preferred_element_type=f32
-    ) + jnp.einsum("jcf,jfd->jcd", up_back, w_up, preferred_element_type=f32)
+    pair_back = jnp.concatenate([gate_back, up_back], axis=2)
+    slot_grad = jnp.einsum("jcf,jfd->jcd", pair_back, w_pair, preferred_element_type=f32)
     back_part = scatter(slot_grad.astype(bf16))
     two_grad = lax.psum_scatter(back_part, "ep", scatter_dimension=0, tiled=True).astype(f32)
     dgate = lax.all_to_all(dgate_own, "ep", split_axis=1, concat_axis=0, tiled=True)
-    in_blocks = column_blocks(dense_in)
-    down_part = shares(inner, column_blocks(dense_grad))
-    gate_part = shares(gate_back, in_blocks)
-    up_part = shares(up_back, in_blocks)
-    two_grad, out_part, down_part, gate_part, up_part = lax.optimization_barrier(
-        (two_grad, out_part, down_part, gate_part, up_part)
-    )
+    half = hidden + hidden // 2
+    down_state = grad_rows(inner, dense_grad, 1)
+    pair_state = grad_rows(pair_back[:, :, :half], dense_in, 2)
+    rest_state = grad_rows(pair_back[:, :, half:], dense_in, 1)
+    out_part = scatter((place_gate * expert_out).astype(bf16))
+    two_grad, out_part = lax.optimization_barrier((two_grad, out_part))
     returned = lax.psum_scatter(out_part, "ep", scatter_dimension=0, tiled=True)
 
     delta = out_cotangent.astype(f32)
@@ -340,10 +350,14 @@
     gain_two_grad = jnp.sum(two_grad * normed_two, axis=0, keepdims=True)
     hidden_grad = delta + norm_back(two_grad, normed_two, scale_two, gain_two)
     hidden_low = hidden_grad.astype(bf16)
-    mixing = jnp.einsum("td,dc->tc", hidden_low, full_out, preferred_element_type=f32)
-    mixing_heads = lax.all_to_all(
-        mixing.astype(bf16), "ep", split_axis=1, concat_axis=0, tiled=True
-    )
+    mixing = jnp.stack(
+        [
+            jnp.einsum("td,dc->tc", hidden_low, part, preferred_element_type=f32).astype(bf16)
+            for part in out_parts
+        ]
+    )
+    mixing = mixing[ordered].transpose(1, 0, 2).reshape(tokens, -1)
+    mixing_heads = lax.all_to_all(mixing, "ep", split_axis=1, concat_axis=0, tiled=True)
     hidden_cols = lax.all_to_all(hidden_low, "ep", split_axis=1, concat_axis=0, tiled=True)
 
     change = mixing_heads.reshape(seq, keys, group, hd).transpose(1, 2, 0, 3)
@@ -381,9 +395,27 @@
     gain_pack = jnp.pad(gain_pack, ((0, 0), (0, 0), (0, width - 2 * gain_width)))
     small_pack = jnp.concatenate([router_grad.reshape(devices, mine, width), gain_pack], axis=1)
     small_pack = lax.all_to_all(small_pack, "ep", split_axis=0, concat_axis=0, tiled=True)
-    small_sum = grp_total(jnp.sum(small_pack, axis=0), copies)
-    qkv_sum = grp_all_sum(qkv_grad.astype(bf16), copies, at)
-    out_sum = grp_all_sum(out_grad.astype(bf16), copies, at)
+    small_part = jnp.sum(small_pack, axis=0)
+    if copies == mine + 1 and grp_direct(copies):
+        per_copy = [
+            qkv_grad.astype(bf16).reshape(copies, -1, width),
+            out_grad.astype(bf16).reshape(copies, -1, width),
+            jnp.pad(small_part.astype(bf16)[:, None], ((0, 0), (0, 7), (0, 0))),
+        ]
+        sizes = [part.shape[1] for part in per_copy]
+        sums = grp_all_sum(
+            jnp.concatenate(per_copy, axis=1).reshape(-1, width), copies, at
+        ).reshape(copies, -1, width)
+        qkv_sum = sums[:, : sizes[0]].reshape(-1, width)
+        out_sum = sums[:, sizes[0] : sizes[0] + sizes[1]].reshape(-1, width)
+        small_sum = sums[:, sizes[0] + sizes[1]]
+    else:
+        qkv_sum = grp_all_sum(qkv_grad.astype(bf16), copies, at)
+        out_sum = grp_all_sum(out_grad.astype(bf16), copies, at)
+        small_sum = grp_total(small_part, copies)
+    down_sum = grad_finish(down_state, 1)
+    pair_sum = grad_finish(pair_state, 2)
+    rest_sum = grad_finish(rest_state, 1)
 
     layer_out = (hidden_one + returned.astype(f32)).astype(bf16)
     residual = layer_in.astype(f32)
@@ -399,9 +431,9 @@
         small_sum[:mine],
         small_sum[mine, :gain_width],
         small_sum[mine, gain_width : 2 * gain_width],
-        grp_sum(gate_part),
-        grp_sum(up_part),
-        grp_sum(down_part),
+        pair_sum[:, :hidden],
+        jnp.concatenate([pair_sum[:, hidden:], rest_sum], axis=1),
+        down_sum,
     )
 
 
@@ -432,4 +464,5 @@
         P("ep", None, "grp"),
         P("ep", None, "grp"),
     )
+
     return jax.shard_map(local, mesh=mesh, in_specs=in_specs, out_specs=out_specs, check_vma=False)

time: 588 us -> 553 us (0.940)
  the two profiles are of different devices: /device:TPU:16 before, /device:TPU:9 now
where the time goes in v3:
time: 553 us; the launch traced here: 543 us
  waiting for transfers between devices  221 us (40%)
  matrix products  120 us (22%)
  starting transfers between devices  71.2 us (13%)
  local copies, waits for them, and re-layouts  56.1 us (10%)
  other arithmetic  43.8 us (8%)
  between operations  16.1 us (3%)
  blocking collectives  14.7 us (3%)
    ppermute x15, waiting for transfers between devices, grp_send(): return lax.ppermute(value, 'grp', [(a, a ^ step) for a in range(copies)])  105 us
    ppermute x10, waiting for transfers between devices, move_blocks(): lax.ppermute(chosen[p], 'ep', pair)  31.7 us
    reduce_scatter x1, waiting for transfers between devices, local(): lax.psum_scatter(back_part, 'ep', scatter_dimension=0, tiled=True)  24 us
    ppermute x10, starting transfers between devices, move_blocks(): lax.ppermute(chosen[p], 'ep', pair)  22.8 us
    unnamed x163, local copies, waits for them, and re-layouts  19.7 us
    all_gather x1, waiting for transfers between devices, local(): x_two_all = lax.all_gather(x_two, 'ep', axis=0, tiled=True)  19.1 us
    all_to_all x1, waiting for transfers between devices, local(): lax.all_to_all(mixed_heads, 'ep', split_axis=0, concat_axis=1, tiled=True)  16.2 us
    dot_general x2, matrix products, scatter(): jnp.einsum('tp,pd->td', pick_back, rows.reshape(mine * capacity, width),...  15.1 us
  transfers between devices with their start and end apart: 38, of which 17 were waited for; matrix products, arithmetic and copies ran while one was open for 28% of the time, Pallas kernels for 0%

profile of v3, /device:TPU:9, one launch (start us, length us, event | category | flops | bytes accessed | tf_op | source)
XLA Modules:
  0.0 543.2 jit_solution(13520750853367123977)
XLA Ops:
  13.2 14.7 %all-gather = bf16[49152]{0:T(1024)(128)(2,1)S(1)} all-gather(bf16[6144]{0:T(1024)(128)(2,1)S(1)} %concatenate.59), channel_id=2, replica_groups=mesh['grp'=4,'ep'=8] {'ep'}, dimensions={0}, use_global_device_ids=true | all-gather | bytes 110592 | tf_op jit(solution)/shard_map/all_gather | solution.py:164
  46.3 18.3 %collective-permute-done.2 = bf16[64,1536]{1,0:T(8,128)(2,1)S(1)} collective-permute-done((bf16[64,1536]{1,0:T(8,128)(2,1)}, bf16[64,1536]{1,0:T(8,128)(2,1)S(1)}, u32[]{:S(2)}, u32[]{:S(2)}) %collective-permute-start.2) | collective-permute-done | bytes 196640 | tf_op jit(solution)/shard_map/ppermute | solution.py:88
  71.3 7.2 %all-gather.7.cloned.1.call-done = bf16[1024,1536]{1,0:T(8,128)(2,1)} async-done(((bf16[128,1536]{1,0:T(8,128)(2,1)}), bf16[1024,1536]{1,0:T(8,128)(2,1)}) %all-gather.7.cloned.1.call-update) | async-done | bytes 3145744 | tf_op jit(solution)/shard_map/all_gather | solution.py:153
  85.4 8.1 %fusion.129 = (f32[3,1024]{1,0:T(4,128)S(1)}, f32[3,1024,1024]{1,2,0:T(8,128)}) fusion(pred[1024,1024]{0,1:T(8,128)(4,1)S(1)} %fusion.13, bf16[1024,64,1]{0,1,2:T(8,128)(2,1)S(1)} %fusion.89, bf16[1024,4,32]{0,2,1:T(8,128)(2,1)S(1)} %get-tuple-element.47, bf16[1024,4,32]{0,2,1:T(8,128)(2,1)S(1)} %get-tuple-element.48), kind=kOutput, calls=%fused_computation.269 | convolution fusion | flops 419169280 | bytes 15347712 | tf_op jit(solution)/shard_map/sub | solution.py:248
  93.5 6.1 %fusion.46 = bf16[3,1024,64]{1,2,0:T(8,128)(2,1)S(1)} fusion(f32[1024,320]{0,1:T(8,128)} %copy-done.40, f32[3,1024,1024]{1,2,0:T(8,128)} %get-tuple-element.75, f32[3,1024]{1,0:T(4,128)S(1)} %get-tuple-element.74), kind=kOutput, calls=%fused_computation.98 | convolution fusion | flops 409141248 | bytes 13119488 | tf_op jit(solution)/shard_map/hgqk,hkd->hgqd/dot_general | solution.py:251
  100.5 6.2 %all-to-all-start = ((bf16[8,128,192]{1,2,0:T(8,128)(2,1)}), bf16[8,128,192]{1,2,0:T(8,128)(2,1)S(1)}, u32[]{:S(2)}, u32[]{:S(2)}) async-start(bf16[8,128,192]{1,2,0:T(8,128)(2,1)} %copy.67), calls=%async_computation | async-start | bytes 786432 | tf_op jit(solution)/shard_map/all_to_all | solution.py:253
  108.1 16.2 %all-to-all-done = bf16[8,128,192]{1,2,0:T(8,128)(2,1)S(1)} async-done(((bf16[8,128,192]{1,2,0:T(8,128)(2,1)}), bf16[8,128,192]{1,2,0:T(8,128)(2,1)S(1)}, u32[]{:S(2)}, u32[]{:S(2)}) %all-to-all-start) | async-done | bytes 393248 | tf_op jit(solution)/shard_map/all_to_all | solution.py:253
  128.5 5.4 collective-permute-done.5
  140.2 5.0 constant_dynamic-update-slice_fusion.1
  147.7 8.1 %convolution_convert_fusion.1 = bf16[1152,1536]{1,0:T(8,128)(2,1)} fusion(pred[1152,1024]{1,0:T(32,128)(4,1)} %bitcast_compare_fusion.1, bf16[1024,1536]{1,0:T(8,128)(2,1)} %all-gather.13.cloned.1.call-done), kind=kOutput, calls=%fused_computation.17 | convolution fusion | flops 3625648128 | bytes 7864320 | tf_op jit(solution)/shard_map/pt,td->pd/dot_general | solution.py:274
  155.8 19.1 %all-gather.11.cloned.1.call-done = bf16[1024,1536]{1,0:T(8,128)(2,1)} async-done(((bf16[128,1536]{1,0:T(8,128)(2,1)}), bf16[1024,1536]{1,0:T(8,128)(2,1)}) %all-gather.11.cloned.1.call-update) | async-done | bytes 3145744 | tf_op jit(solution)/shard_map/all_gather | solution.py:262
  174.9 5.9 %convolution_convert_fusion = bf16[1152,1536]{1,0:T(8,128)(2,1)S(1)} fusion(pred[1152,1024]{1,0:T(32,128)(4,1)S(1)} %copy-done.37, bf16[1024,1536]{1,0:T(8,128)(2,1)} %all-gather.11.cloned.1.call-done), kind=kOutput, calls=%fused_computation.16 | convolution fusion | flops 3625648128 | bytes 7864320 | tf_op jit(solution)/shard_map/pt,td->pd/dot_general | solution.py:274
  182.7 7.2 %fusion.135 = f32[3,384,1024]{2,1,0:T(8,128)S(1)} fusion(bf16[3,384,1536]{2,1,0:T(8,128)(2,1)S(1)} %bitcast.272, bf16[3,1024,1536]{2,1,0:T(8,128)(2,1)} %constant_dynamic-update-slice_fusion), kind=kOutput, calls=%fused_computation.271 | convolution fusion | flops 3623878656 | bytes 17694720 | tf_op jit(solution)/shard_map/jcd,jfd->jcf/dot_general | solution.py:318
  203.6 8.7 %convolution_convert_fusion.2 = bf16[3,384,1536]{2,1,0:T(8,128)(2,1)S(1)} fusion(bf16[3,1024,1536]{2,1,0:T(8,128)(2,1)} %constant_dynamic-update-slice_fusion, bf16[3,384,512]{2,1,0:T(8,128)(2,1)S(1)} %get-tuple-element.31, bf16[3,384,512]{2,1,0:T(8,128)(2,1)S(1)} %get-tuple-element.30), kind=kOutput, calls=%fused_computation.42 | convolution fusion | flops 3630366720 | bytes 15335424 | tf_op jit(solution)/shard_map/jcf,jfd->jcd/dot_general | solution.py:330
  212.3 6.1 %convolution_convert_fusion.4 = bf16[1024,1536]{1,0:T(8,128)(2,1)} fusion(bf16[1024,1152]{0,1:T(8,128)(2,1)S(1)} %copy-done.32, bf16[1152,1536]{1,0:T(8,128)(2,1)S(1)} %bitcast.301), kind=kOutput, calls=%fused_computation.44 | convolution fusion | flops 3625451520 | bytes 9043968 | tf_op jit(solution)/shard_map/tp,pd->td/dot_general | solution.py:278
  218.5 4.5 all-to-all-start.1
  223.0 8.9 %convolution_convert_fusion.3 = bf16[1024,1536]{1,0:T(8,128)(2,1)} fusion(bf16[1024,1152]{0,1:T(8,128)(2,1)} %fusion.12, bf16[1152,1536]{1,0:T(8,128)(2,1)} %bitcast.266), kind=kOutput, calls=%fused_computation.43 | convolution fusion | flops 3625451520 | bytes 9043968 | tf_op jit(solution)/shard_map/tp,pd->td/dot_general | solution.py:278
  232.0 24.0 %reduce-scatter.4.cloned.1.call-done = bf16[128,1536]{1,0:T(8,128)(2,1)} async-done(((bf16[1024,1536]{1,0:T(8,128)(2,1)}), bf16[128,1536]{1,0:T(8,128)(2,1)}) %reduce-scatter.4.cloned.1.call-update) | async-done | bytes 393232 | tf_op jit(solution)/shard_map/reduce_scatter | solution.py:332
  265.8 6.6 %all-to-all-start.2 = ((bf16[128,8,192]{0,2,1:T(8,128)(2,1)}), bf16[128,8,192]{0,2,1:T(8,128)(2,1)S(1)}, u32[]{:S(2)}, u32[]{:S(2)}) async-start(bf16[128,8,192]{0,2,1:T(8,128)(2,1)} %bitcast.281), calls=%async_computation.4 | async-start | bytes 786432 | tf_op jit(solution)/shard_map/all_to_all | solution.py:360
  273.0 8.6 %all-to-all-done.2 = bf16[128,8,192]{0,2,1:T(8,128)(2,1)S(1)} async-done(((bf16[128,8,192]{0,2,1:T(8,128)(2,1)}), bf16[128,8,192]{0,2,1:T(8,128)(2,1)S(1)}, u32[]{:S(2)}, u32[]{:S(2)}) %all-to-all-start.2) | async-done | bytes 393248 | tf_op jit(solution)/shard_map/all_to_all | solution.py:360
  283.8 6.1 %multiply_reduce_fusion = (f32[3,1024]{1,0:T(4,128)S(1)}, f32[3,1024,1024]{1,2,0:T(8,128)S(1)}) fusion(f32[3,1024,1024]{1,2,0:T(8,128)} %get-tuple-element.75, f32[3,1024]{1,0:T(4,128)S(1)} %copy-done.54, f32[1024,320]{0,1:T(8,128)} %copy-done.40, bf16[1024,1,3,64]{0,3,2,1:T(8,128)(2,1)S(1)} %reshape.491), kind=kOutput, calls=%fused_computation.8 | convolution fusion | flops 412087296 | bytes 25714688 | tf_op jit(solution)/shard_map/hgqd,hkd->hgqk/dot_general | solution.py:364
  289.9 7.7 %multiply_convert_fusion = bf16[3,1024,1024]{1,2,0:T(8,128)(2,1)S(1)} fusion(f32[3,1024,1024]{1,2,0:T(8,128)S(1)} %get-tuple-element.84, f32[3,1024]{1,0:T(4,128)S(1)} %get-tuple-element.83, f32[3,1024,1024]{1,2,0:T(8,128)} %get-tuple-element.75, f32[3,1024]{1,0:T(4,128)S(1)} %copy-done.54), kind=kLoop, calls=%fused_computation.7 | loop fusion | flops 12582912 | bytes 31481856 | tf_op jit(solution)/shard_map/convert_element_type | solution.py:366
  303.6 4.4 fusion.7
  326.3 72.1 %collective-permute-done.21 = bf16[3,256,768]{2,1,0:T(8,128)(2,1)} collective-permute-done((bf16[3,256,768]{2,1,0:T(8,128)(2,1)}, bf16[3,256,768]{2,1,0:T(8,128)(2,1)}, u32[]{:S(2)}, u32[]{:S(2)}) %collective-permute-start.21) | collective-permute-done | bytes 1179680 | tf_op jit(solution)/shard_map/ppermute | solution.py:96
  410.4 4.6 convert_add_fusion
  421.5 8.5 %all-to-all-start.3 = ((bf16[128,8,192]{0,2,1:T(8,128)(2,1)}), bf16[128,8,192]{0,2,1:T(8,128)(2,1)S(1)}, u32[]{:S(2)}, u32[]{:S(2)}) async-start(bf16[128,8,192]{0,2,1:T(8,128)(2,1)} %bitcast.80), calls=%async_computation.6 | async-start | bytes 786432 | tf_op jit(solution)/shard_map/all_to_all | solution.py:361
  437.7 8.4 %all-to-all-done.3 = bf16[128,8,192]{0,2,1:T(8,128)(2,1)S(1)} async-done(((bf16[128,8,192]{0,2,1:T(8,128)(2,1)}), bf16[128,8,192]{0,2,1:T(8,128)(2,1)S(1)}, u32[]{:S(2)}, u32[]{:S(2)}) %all-to-all-start.3) | async-done | bytes 393248 | tf_op jit(solution)/shard_map/all_to_all | solution.py:361
  446.1 7.8 %all-to-all-start.4 = ((f32[8,4,1536]{2,1,0:T(4,128)}), f32[8,4,1536]{2,1,0:T(4,128)S(1)}, u32[]{:S(2)}, u32[]{:S(2)}) async-start(f32[8,4,1536]{2,1,0:T(4,128)} %select_maximum_fusion), calls=%async_computation.7 | async-start | bytes 393216 | tf_op jit(solution)/shard_map/all_to_all | solution.py:397
  462.7 5.4 collective-permute-done.10
  470.1 5.2 collective-permute-done.12
  490.9 11.3 %collective-permute-done.14 = bf16[136,1536]{1,0:T(8,128)(2,1)S(1)} collective-permute-done((bf16[136,1536]{1,0:T(8,128)(2,1)S(1)}, bf16[136,1536]{1,0:T(8,128)(2,1)S(1)}, u32[]{:S(2)}, u32[]{:S(2)}) %collective-permute-start.14) | collective-permute-done | bytes 417824 | tf_op jit(solution)/shard_map/ppermute | solution.py:96
  514.2 9.8 %collective-permute-done.17 = bf16[136,1536]{1,0:T(8,128)(2,1)S(1)} collective-permute-done((bf16[136,1536]{1,0:T(8,128)(2,1)S(1)}, bf16[136,1536]{1,0:T(8,128)(2,1)S(1)}, u32[]{:S(2)}, u32[]{:S(2)}) %collective-permute-start.17) | collective-permute-done | bytes 417824 | tf_op jit(solution)/shard_map/ppermute | solution.py:96
  (359 shorter events, 180.8 us)
Async XLA Ops:
  7.2 61.9 %all-gather.9.cloned.1.call-start = ((), (), s32[]{:S(2)}) async-start(), calls=%async_computation.9 | async-start | bytes 1327104 | tf_op jit(solution)/shard_map/all_gather | solution.py:195
  8.9 69.6 %all-gather.7.cloned.1.call-start = ((), (), s32[]{:S(2)}) async-start(), calls=%async_computation.8 | async-start | bytes 3538944 | tf_op jit(solution)/shard_map/all_gather | solution.py:153
  9.7 138.0 %all-gather.13.cloned.1.call-start = ((), (), s32[]{:S(2)}) async-start(), calls=%async_computation.11 | async-start | bytes 3538944 | tf_op jit(solution)/shard_map/all_gather | solution.py:207
  31.4 13.9 %collective-permute-start = (bf16[64,1536]{1,0:T(8,128)(2,1)S(1)}, bf16[64,1536]{1,0:T(8,128)(2,1)}, u32[]{:S(2)}, u32[]{:S(2)}) collective-permute-start(bf16[64,1536]{1,0:T(8,128)(2,1)S(1)} %get-tuple-element.53), channel_id=1, source_target_pairs={{0,0},{1,2},{2,4},{3,5},{4,7},{5,1},{6,6},{7,3},{8,8},{9,10},{10,1... | collective-permute-start | bytes 589832 | tf_op jit(solution)/shard_map/ppermute | solution.py:88
  36.9 27.8 %collective-permute-start.2 = (bf16[64,1536]{1,0:T(8,128)(2,1)}, bf16[64,1536]{1,0:T(8,128)(2,1)S(1)}, u32[]{:S(2)}, u32[]{:S(2)}) collective-permute-start(bf16[64,1536]{1,0:T(8,128)(2,1)} %get-tuple-element.51), channel_id=1, source_target_pairs={{0,1},{1,2},{2,4},{3,6},{4,7},{5,3},{6,0},{7,5},{8,9},{9,10},{10,1... | collective-permute-start | bytes 589832 | tf_op jit(solution)/shard_map/ppermute | solution.py:88
  38.1 26.6 %collective-permute-start.3 = (bf16[64,1536]{1,0:T(8,128)(2,1)}, bf16[64,1536]{1,0:T(8,128)(2,1)S(1)}, u32[]{:S(2)}, u32[]{:S(2)}) collective-permute-start(bf16[64,1536]{1,0:T(8,128)(2,1)} %get-tuple-element.50), channel_id=1, source_target_pairs={{0,0},{1,2},{2,3},{3,5},{4,7},{5,4},{6,1},{7,6},{8,8},{9,10},{10,1... | collective-permute-start | bytes 589832 | tf_op jit(solution)/shard_map/ppermute | solution.py:88
  40.3 27.1 %collective-permute-start.4 = (bf16[64,1536]{1,0:T(8,128)(2,1)}, bf16[64,1536]{1,0:T(8,128)(2,1)S(1)}, u32[]{:S(2)}, u32[]{:S(2)}) collective-permute-start(bf16[64,1536]{1,0:T(8,128)(2,1)} %get-tuple-element.49), channel_id=1, source_target_pairs={{0,1},{1,3},{2,4},{3,6},{4,0},{5,5},{6,2},{7,7},{8,9},{9,11},{10,1... | collective-permute-start | bytes 589832 | tf_op jit(solution)/shard_map/ppermute | solution.py:88
  69.1 39.0 %collective-permute-start.7 = (bf16[1536,384]{1,0:T(8,128)(2,1)}, bf16[1536,384]{1,0:T(8,128)(2,1)}, u32[]{:S(2)}, u32[]{:S(2)}) collective-permute-start(bf16[1536,384]{1,0:T(8,128)(2,1)} %all-gather.9.cloned.1.call-done), channel_id=1, source_target_pairs={{0,24},{8,16},{16,8},{24,0},{1,25},{9,17},{17,9},{25,1},{2,26},{10... | collective-permute-start | bytes 3538952 | tf_op jit(solution)/shard_map/ppermute | solution.py:96
  71.3 54.8 %collective-permute-start.6 = (bf16[1536,384]{1,0:T(8,128)(2,1)}, bf16[1536,384]{1,0:T(8,128)(2,1)}, u32[]{:S(2)}, u32[]{:S(2)}) collective-permute-start(bf16[1536,384]{1,0:T(8,128)(2,1)} %all-gather.9.cloned.1.call-done), channel_id=1, source_target_pairs={{0,16},{8,24},{16,0},{24,8},{1,17},{9,25},{17,1},{25,9},{2,18},{10... | collective-permute-start | bytes 3538952 | tf_op jit(solution)/shard_map/ppermute | solution.py:96
  100.5 23.7 %all-to-all-start = ((bf16[8,128,192]{1,2,0:T(8,128)(2,1)}), bf16[8,128,192]{1,2,0:T(8,128)(2,1)S(1)}, u32[]{:S(2)}, u32[]{:S(2)}) async-start(bf16[8,128,192]{1,2,0:T(8,128)(2,1)} %copy.67), calls=%async_computation | async-start | bytes 786432 | tf_op jit(solution)/shard_map/all_to_all | solution.py:253
  106.7 68.2 %all-gather.11.cloned.1.call-start = ((), (), s32[]{:S(2)}) async-start(), calls=%async_computation.10 | async-start | bytes 3538944 | tf_op jit(solution)/shard_map/all_gather | solution.py:262
  106.7 27.2 %collective-permute-start.5 = (bf16[1536,384]{1,0:T(8,128)(2,1)S(1)}, bf16[1536,384]{1,0:T(8,128)(2,1)S(1)}, u32[]{:S(2)}, u32[]{:S(2)}) collective-permute-start(bf16[1536,384]{1,0:T(8,128)(2,1)S(1)} %copy-done.13), channel_id=1, source_target_pairs={{0,8},{8,0},{16,24},{24,16},{1,9},{9,1},{17,25},{25,17},{2,10},{10... | collective-permute-start | bytes 3538952 | tf_op jit(solution)/shard_map/ppermute | solution.py:96
  135.5 120.5 %reduce-scatter.4.cloned.1.call-start = ((), (), s32[]{:S(2)}) async-start(), calls=%async_computation.12 | async-start | bytes 3538944 | tf_op jit(solution)/shard_map/reduce_scatter | solution.py:332
  218.5 13.5 %all-to-all-start.1 = ((f32[3,8,128]{2,0,1:T(4,128)}), f32[3,8,128]{2,0,1:T(4,128)S(1)}, u32[]{:S(2)}, u32[]{:S(2)}) async-start(f32[3,8,128]{2,0,1:T(4,128)} %bitcast.40), calls=%async_computation.3 | async-start | bytes 32768 | tf_op jit(solution)/shard_map/all_to_all | solution.py:333
  265.8 15.8 %all-to-all-start.2 = ((bf16[128,8,192]{0,2,1:T(8,128)(2,1)}), bf16[128,8,192]{0,2,1:T(8,128)(2,1)S(1)}, u32[]{:S(2)}, u32[]{:S(2)}) async-start(bf16[128,8,192]{0,2,1:T(8,128)(2,1)} %bitcast.281), calls=%async_computation.4 | async-start | bytes 786432 | tf_op jit(solution)/shard_map/all_to_all | solution.py:360
  272.4 181.6 %all-gather.15.cloned.1.call-start = ((), (), s32[]{:S(2)}) async-start(), calls=%async_computation.15 | async-start | bytes 3538944 | tf_op jit(solution)/shard_map/all_gather | solution.py:264
  273.0 258.6 %reduce-scatter.8.cloned.1.call-start = ((), (), s32[]{:S(2)}) async-start(), calls=%async_computation.14 | async-start | bytes 3538944 | tf_op jit(solution)/shard_map/reduce_scatter | solution.py:383
  308.1 224.9 %reduce-scatter.6.cloned.1.call-start = ((), (), s32[]{:S(2)}) async-start(), calls=%async_computation.13 | async-start | bytes 3538944 | tf_op jit(solution)/shard_map/reduce_scatter | solution.py:340
  315.8 94.6 %collective-permute-start.19 = (bf16[3,768,768]{2,1,0:T(8,128)(2,1)}, bf16[3,768,768]{2,1,0:T(8,128)(2,1)}, u32[]{:S(2)}, u32[]{:S(2)}) collective-permute-start(bf16[3,768,768]{2,1,0:T(8,128)(2,1)} %convolution_convert_fusion.7), channel_id=1, source_target_pairs={{0,16},{8,24},{16,0},{24,8},{1,17},{9,25},{17,1},{25,9},{2,18},{10... | collective-permute-start | bytes 10616840 | tf_op jit(solution)/shard_map/ppermute | solution.py:96
  321.5 81.2 %collective-permute-start.23 = (bf16[3,512,768]{2,1,0:T(8,128)(2,1)}, bf16[3,512,768]{2,1,0:T(8,128)(2,1)}, u32[]{:S(2)}, u32[]{:S(2)}) collective-permute-start(bf16[3,512,768]{2,1,0:T(8,128)(2,1)} %convolution_convert_fusion.8), channel_id=1, source_target_pairs={{0,8},{8,0},{16,24},{24,16},{1,9},{9,1},{17,25},{25,17},{2,10},{10... | collective-permute-start | bytes 7077896 | tf_op jit(solution)/shard_map/ppermute | solution.py:96
  324.5 73.9 %collective-permute-start.21 = (bf16[3,256,768]{2,1,0:T(8,128)(2,1)}, bf16[3,256,768]{2,1,0:T(8,128)(2,1)}, u32[]{:S(2)}, u32[]{:S(2)}) collective-permute-start(bf16[3,256,768]{2,1,0:T(8,128)(2,1)} %fusion.42), channel_id=1, source_target_pairs={{0,8},{8,0},{16,24},{24,16},{1,9},{9,1},{17,25},{25,17},{2,10},{10... | collective-permute-start | bytes 3538952 | tf_op jit(solution)/shard_map/ppermute | solution.py:96
  402.3 80.5 %collective-permute-start.22 = (bf16[3,256,384]{2,1,0:T(8,128)(2,1)}, bf16[3,256,384]{2,1,0:T(8,128)(2,1)}, u32[]{:S(2)}, u32[]{:S(2)}) collective-permute-start(bf16[3,256,384]{2,1,0:T(8,128)(2,1)} %slice.333), channel_id=1, source_target_pairs={{0,16},{8,24},{16,0},{24,8},{1,17},{9,25},{17,1},{25,9},{2,18},{10... | collective-permute-start | bytes 1769480 | tf_op jit(solution)/shard_map/ppermute | solution.py:96
  409.4 75.5 %collective-permute-start.24 = (bf16[3,512,384]{2,1,0:T(8,128)(2,1)}, bf16[3,512,384]{2,1,0:T(8,128)(2,1)}, u32[]{:S(2)}, u32[]{:S(2)}) collective-permute-start(bf16[3,512,384]{2,1,0:T(8,128)(2,1)} %slice.332), channel_id=1, source_target_pairs={{0,16},{8,24},{16,0},{24,8},{1,17},{9,25},{17,1},{25,9},{2,18},{10... | collective-permute-start | bytes 3538952 | tf_op jit(solution)/shard_map/ppermute | solution.py:96
  419.3 85.9 %collective-permute-start.20 = (bf16[3,768,384]{2,1,0:T(8,128)(2,1)}, bf16[3,768,384]{2,1,0:T(8,128)(2,1)}, u32[]{:S(2)}, u32[]{:S(2)}) collective-permute-start(bf16[3,768,384]{2,1,0:T(8,128)(2,1)} %slice.331), channel_id=1, source_target_pairs={{0,8},{8,0},{16,24},{24,16},{1,9},{9,1},{17,25},{25,17},{2,10},{10... | collective-permute-start | bytes 5308424 | tf_op jit(solution)/shard_map/ppermute | solution.py:96
  421.5 24.7 %all-to-all-start.3 = ((bf16[128,8,192]{0,2,1:T(8,128)(2,1)}), bf16[128,8,192]{0,2,1:T(8,128)(2,1)S(1)}, u32[]{:S(2)}, u32[]{:S(2)}) async-start(bf16[128,8,192]{0,2,1:T(8,128)(2,1)} %bitcast.80), calls=%async_computation.6 | async-start | bytes 786432 | tf_op jit(solution)/shard_map/all_to_all | solution.py:361
  431.0 26.0 %collective-permute-start.8 = (bf16[64,1024]{1,0:T(8,128)(2,1)S(1)}, bf16[64,1024]{1,0:T(8,128)(2,1)S(1)}, u32[]{:S(2)}, u32[]{:S(2)}) collective-permute-start(bf16[64,1024]{1,0:T(8,128)(2,1)S(1)} %get-tuple-element.60), channel_id=1, source_target_pairs={{0,0},{2,1},{4,2},{5,3},{7,4},{1,5},{6,6},{3,7},{8,8},{10,9},{12,1... | collective-permute-start | bytes 393224 | tf_op jit(solution)/shard_map/ppermute | solution.py:88
  435.0 24.8 %collective-permute-start.9 = (bf16[64,1024]{1,0:T(8,128)(2,1)S(1)}, bf16[64,1024]{1,0:T(8,128)(2,1)}, u32[]{:S(2)}, u32[]{:S(2)}) collective-permute-start(bf16[64,1024]{1,0:T(8,128)(2,1)S(1)} %get-tuple-element.59), channel_id=1, source_target_pairs={{0,0},{1,1},{3,2},{5,3},{6,4},{2,5},{7,6},{4,7},{8,8},{9,9},{11,10... | collective-permute-start | bytes 393224 | tf_op jit(solution)/shard_map/ppermute | solution.py:88
  446.1 34.2 %all-to-all-start.4 = ((f32[8,4,1536]{2,1,0:T(4,128)}), f32[8,4,1536]{2,1,0:T(4,128)S(1)}, u32[]{:S(2)}, u32[]{:S(2)}) async-start(f32[8,4,1536]{2,1,0:T(4,128)} %select_maximum_fusion), calls=%async_computation.7 | async-start | bytes 393216 | tf_op jit(solution)/shard_map/all_to_all | solution.py:397
  482.1 20.0 %collective-permute-start.14 = (bf16[136,1536]{1,0:T(8,128)(2,1)S(1)}, bf16[136,1536]{1,0:T(8,128)(2,1)S(1)}, u32[]{:S(2)}, u32[]{:S(2)}) collective-permute-start(bf16[136,1536]{1,0:T(8,128)(2,1)S(1)} %get-tuple-element.44), channel_id=1, source_target_pairs={{0,16},{8,24},{16,0},{24,8},{1,17},{9,25},{17,1},{25,9},{2,18},{10... | collective-permute-start | bytes 1253384 | tf_op jit(solution)/shard_map/ppermute | solution.py:96
  482.9 19.3 %collective-permute-start.13 = (bf16[136,1536]{1,0:T(8,128)(2,1)S(1)}, bf16[136,1536]{1,0:T(8,128)(2,1)S(1)}, u32[]{:S(2)}, u32[]{:S(2)}) collective-permute-start(bf16[136,1536]{1,0:T(8,128)(2,1)S(1)} %get-tuple-element.42), channel_id=1, source_target_pairs={{0,8},{8,0},{16,24},{24,16},{1,9},{9,1},{17,25},{25,17},{2,10},{10... | collective-permute-start | bytes 1253384 | tf_op jit(solution)/shard_map/ppermute | solution.py:96
  503.9 20.0 %collective-permute-start.17 = (bf16[136,1536]{1,0:T(8,128)(2,1)S(1)}, bf16[136,1536]{1,0:T(8,128)(2,1)S(1)}, u32[]{:S(2)}, u32[]{:S(2)}) collective-permute-start(bf16[136,1536]{1,0:T(8,128)(2,1)S(1)} %fusion.70), channel_id=1, source_target_pairs={{0,16},{8,24},{16,0},{24,8},{1,17},{9,25},{17,1},{25,9},{2,18},{10... | collective-permute-start | bytes 1253384 | tf_op jit(solution)/shard_map/ppermute | solution.py:96
  504.6 19.3 %collective-permute-start.16 = (bf16[136,1536]{1,0:T(8,128)(2,1)S(1)}, bf16[136,1536]{1,0:T(8,128)(2,1)S(1)}, u32[]{:S(2)}, u32[]{:S(2)}) collective-permute-start(bf16[136,1536]{1,0:T(8,128)(2,1)S(1)} %fusion.70), channel_id=1, source_target_pairs={{0,8},{8,0},{16,24},{24,16},{1,9},{9,1},{17,25},{25,17},{2,10},{10... | collective-permute-start | bytes 1253384 | tf_op jit(solution)/shard_map/ppermute | solution.py:96
  (82 other events, 859.3 us)
Sparse Core Ops, SparseCore 0:
  10.2 24.5 all-gather.8
  36.5 42.0 all-gather.6
  81.3 44.8 all-gather.12
  135.6 39.2 all-gather.10
  218.6 37.4 reduce-scatter.3
  274.5 38.4 all-gather.14
  315.3 37.8 reduce-scatter.7
  410.5 63.8 reduce-scatter.5
